TPU v7x, 128 devices: a whole 4x4x4 slice. The times are simulated.
128 devices in a mesh: fsdp: 4 (over z_hi, core), seq: 32 (over x, z_lo, y).
Axes of the slice: x: 4, y: 4, z: 4 (z_hi: 2, z_lo: 2; z = z_hi * 2 + z_lo), core: 2. Of those that a mesh axis runs over, the one named last changes fastest.
Arguments:
- stream_in: bfloat16 [16384, 1536], P(('fsdp', 'seq')), may hold values from -6 to 6
- queries: bfloat16 [16384, 768], P(('fsdp', 'seq')), may hold values from -6 to 6
- key_proj: bfloat16 [16384, 768], P(('fsdp', 'seq')), may hold values from -6 to 6
- values: bfloat16 [16384, 768], P(('fsdp', 'seq')), may hold values from -6 to 6
- w_out: bfloat16 [768, 1536], P('fsdp'), may hold values from -0.21875 to 0.21875
- conv_kernel: bfloat16 [32, 1536], P('fsdp'), may hold values from -1 to 1
- valid_length: int32 [1], replicated, may hold values from 15360 to 16384
- grad_out: bfloat16 [16384, 1536], P(('fsdp', 'seq')), may hold values from -6 to 6
Outputs:
- block_out: bfloat16 [16384, 1536], P(('fsdp', 'seq'))
- grad_stream: bfloat16 [16384, 1536], P(('fsdp', 'seq'))
- grad_queries: bfloat16 [16384, 768], P(('fsdp', 'seq'))
- grad_keys: bfloat16 [16384, 768], P(('fsdp', 'seq'))
- grad_values: bfloat16 [16384, 768], P(('fsdp', 'seq'))
- grad_w_out: float32 [768, 1536], P('fsdp')
- grad_kernel: float32 [32, 1536], P('fsdp')
Inputs may be any that keep to these rules, and one draw needn't show every extreme that they name: Frames from valid_length on are padding.
All inputs are finite; a program needn't handle non-finite values.
Results may differ from a plain program's by a relative error of at most 0.02.
Values may be sent and summed in bfloat16 or wider, within the bound.
No kernel may reach another device: no remote copies, remote signals or barrier semaphores. Data moves between devices by JAX's collectives and lax.ppermute only.
A program may use at most 128 MiB of HBM per device.

v0:
```python
import jax
import jax.numpy as jnp
from jax import lax
from jax.sharding import PartitionSpec as P

HEADS = 8
HEAD = 96
TAPS = 32
WIN = 1024


NEG_BIG = -1e30


def shifted_2(value, axis, steps):
    count = lax.axis_size(axis)
    initial, last = (max(0, -steps), min(count, count - steps))
    return lax.ppermute(value, axis, [(source, source + steps) for source in range(initial, last)])


def padded(block, sides, width):
    for axis, dim in sides:
        count = lax.axis_size(axis)
        forward = [(i, i + 1) for i in range(count - 1)]
        backward = [(target, source) for source, target in forward]
        low = lax.ppermute(
            lax.slice_in_dim(block, block.shape[dim] - width, None, axis=dim), axis, forward
        )
        high = lax.ppermute(lax.slice_in_dim(block, 0, width, axis=dim), axis, backward)
        block = jnp.concatenate([low, block, high], axis=dim)
    return block


def band_probs(query_pos, key_pos, query_part, key_part, valid_limit, head_count):
    frames = query_part.shape[0]
    span_len = key_part.shape[0]
    visible = (
        (jnp.abs(query_pos[:, None] - key_pos[None, :]) <= WIN)
        & (key_pos[None, :] >= 0)
        & (key_pos[None, :] < valid_limit)
    )
    query_heads = query_part.reshape(frames, head_count, HEAD)
    key_heads = key_part.reshape(span_len, head_count, HEAD)
    scores = jnp.einsum(
        "qhe,khe->hqk", query_heads, key_heads, preferred_element_type=jnp.float32
    ) * HEAD ** (-0.5)
    scores = jnp.where(visible[None], scores, NEG_BIG)
    top_score = jnp.max(scores, axis=-1, keepdims=True)
    exp_total = jnp.sum(
        jnp.where(visible[None], jnp.exp(scores - top_score), 0.0), axis=-1, keepdims=True
    )
    log_total = top_score + jnp.log(exp_total)
    return jnp.where(visible[None], jnp.exp(scores - log_total), 0.0)


def add_pairs(earlier, later):
    return (earlier[0] + later[0], earlier[1] + later[1])


def per_device(stream_in, queries, key_proj, values, w_out, conv_kernel, valid_length, grad_out):
    frames = queries.shape[0]
    reach_dev = WIN // frames
    span_len = frames * (2 * reach_dev + 1)
    half_taps = TAPS // 2
    score_scale = HEAD ** (-0.5)
    device_index = lax.axis_index(("fsdp", "seq"))
    valid_limit = valid_length[0]
    weight_full, kernel_full = (
        lax.all_gather(w_out, "fsdp", axis=0, tiled=True),
        lax.all_gather(conv_kernel, "fsdp", axis=0, tiled=True),
    )
    own_pair = (key_proj, values)
    offsets = [reach_dev - position for position in range(2 * reach_dev + 1)]
    received = {0: own_pair}
    for direction in (1, -1):
        moving = own_pair
        for distance in range(1, reach_dev + 1):
            moving = shifted_2((moving[0], moving[1]), ("fsdp", "seq"), direction)
            received[direction * distance] = moving
    key_window = jnp.concatenate([received[offset][0] for offset in offsets], axis=0)
    value_window = jnp.concatenate([received[offset][1] for offset in offsets], axis=0)
    query_pos = device_index * frames + jnp.arange(frames, dtype=jnp.int32)
    key_pos = (device_index - reach_dev) * frames + jnp.arange(span_len, dtype=jnp.int32)
    group_heads = 4
    group_width = group_heads * HEAD
    group_count = HEADS // group_heads
    context_parts = []
    for group_index in range(group_count):
        column_slice = slice(group_index * group_width, (group_index + 1) * group_width)
        attn_weights = band_probs(
            query_pos,
            key_pos,
            queries[:, column_slice],
            key_window[:, column_slice],
            valid_limit,
            group_heads,
        ).astype(jnp.bfloat16)
        value_heads = value_window[:, column_slice].reshape(span_len, group_heads, HEAD)
        context_part = jnp.einsum(
            "hqk,khe->qhe", attn_weights, value_heads, preferred_element_type=jnp.float32
        )
        context_parts.append(context_part.reshape(frames, group_width))
    context = jnp.concatenate(context_parts, axis=1).astype(jnp.bfloat16)
    attended = jnp.dot(context, weight_full, preferred_element_type=jnp.float32)
    mixed_in = stream_in.astype(jnp.float32) + attended
    live_rows = (query_pos < valid_limit)[:, None]
    masked = jnp.where(live_rows, mixed_in, 0.0).astype(jnp.bfloat16)
    masked_ext = padded(masked, ((("fsdp", "seq"), 0),), half_taps).astype(jnp.float32)
    grad_ext = padded(grad_out, ((("fsdp", "seq"), 0),), half_taps).astype(jnp.float32)
    kernel = kernel_full.astype(jnp.float32)
    grad_float = grad_out.astype(jnp.float32)
    conv_sum = jnp.zeros((frames, stream_in.shape[1]), jnp.float32)
    conv_back = jnp.zeros((frames, stream_in.shape[1]), jnp.float32)
    kernel_rows = []
    for tap_index in range(TAPS):
        shifted = masked_ext[tap_index : tap_index + frames]
        conv_sum = conv_sum + kernel[tap_index] * shifted
        conv_back = (
            conv_back
            + kernel[tap_index]
            * grad_ext[2 * half_taps - tap_index : 2 * half_taps - tap_index + frames]
        )
        kernel_rows.append(jnp.sum(grad_float * shifted, axis=0))
    block_out = (mixed_in + conv_sum).astype(jnp.bfloat16)
    grad_stream = (grad_float + jnp.where(live_rows, conv_back, 0.0)).astype(jnp.bfloat16)
    term_kernel = jnp.stack(kernel_rows)
    term_weight = lax.dot_general(
        context, grad_stream, (((0,), (0,)), ((), ())), preferred_element_type=jnp.float32
    )
    summed = lax.psum((term_weight, term_kernel), "seq")
    grad_w_out, grad_kernel = (
        lax.psum_scatter(summed[0], "fsdp", scatter_dimension=0, tiled=True),
        lax.psum_scatter(summed[1], "fsdp", scatter_dimension=0, tiled=True),
    )
    grad_context = lax.dot_general(
        grad_stream, weight_full, (((1,), (1,)), ((), ())), preferred_element_type=jnp.float32
    ).astype(jnp.bfloat16)
    row_delta = jnp.sum(
        (grad_context.astype(jnp.float32) * context.astype(jnp.float32)).reshape(
            frames, HEADS, HEAD
        ),
        axis=-1,
    )
    query_grad_parts = []
    key_grad_parts = []
    value_grad_parts = []
    for group_index in range(group_count):
        column_slice = slice(group_index * group_width, (group_index + 1) * group_width)
        attn_probs = band_probs(
            query_pos,
            key_pos,
            queries[:, column_slice],
            key_window[:, column_slice],
            valid_limit,
            group_heads,
        )
        attn_weights = attn_probs.astype(jnp.bfloat16)
        grad_heads = grad_context[:, column_slice].reshape(frames, group_heads, HEAD)
        value_heads = value_window[:, column_slice].reshape(span_len, group_heads, HEAD)
        grad_probs = jnp.einsum(
            "qhe,khe->hqk", grad_heads, value_heads, preferred_element_type=jnp.float32
        )
        delta_part = jnp.transpose(
            row_delta[:, group_index * group_heads : (group_index + 1) * group_heads]
        )
        grad_scores = (attn_probs * (grad_probs - delta_part[:, :, None])).astype(jnp.bfloat16)
        key_heads = key_window[:, column_slice].reshape(span_len, group_heads, HEAD)
        query_heads = queries[:, column_slice].reshape(frames, group_heads, HEAD)
        grad_query = (
            jnp.einsum("hqk,khe->qhe", grad_scores, key_heads, preferred_element_type=jnp.float32)
            * score_scale
        )
        grad_key = (
            jnp.einsum("hqk,qhe->khe", grad_scores, query_heads, preferred_element_type=jnp.float32)
            * score_scale
        )
        grad_value = jnp.einsum(
            "hqk,qhe->khe", attn_weights, grad_heads, preferred_element_type=jnp.float32
        )
        query_grad_parts.append(grad_query.reshape(frames, group_width))
        key_grad_parts.append(grad_key.reshape(span_len, group_width))
        value_grad_parts.append(grad_value.reshape(span_len, group_width))
    grad_queries = jnp.concatenate(query_grad_parts, axis=1).astype(jnp.bfloat16)
    key_grad_window = jnp.concatenate(key_grad_parts, axis=1)
    value_grad_window = jnp.concatenate(value_grad_parts, axis=1)
    pieces = {}
    for offset in offsets:
        position = reach_dev - offset
        pieces[offset] = (
            key_grad_window[position * frames : (position + 1) * frames],
            value_grad_window[position * frames : (position + 1) * frames],
        )
    collected = pieces[0]
    for direction in (1, -1):
        running = pieces[direction * reach_dev]
        for distance in range(reach_dev - 1, -1, -1):
            running = shifted_2(running, ("fsdp", "seq"), -direction)
            if distance > 0:
                running = add_pairs(running, pieces[direction * distance])
        collected = add_pairs(collected, running)
    grad_keys = collected[0].astype(jnp.bfloat16)
    grad_values = collected[1].astype(jnp.bfloat16)
    return (block_out, grad_stream, grad_queries, grad_keys, grad_values, grad_w_out, grad_kernel)


def solution(mesh):
    return jax.shard_map(
        per_device,
        mesh=mesh,
        in_specs=(
            P(("fsdp", "seq"), None),
            P(("fsdp", "seq"), None),
            P(("fsdp", "seq"), None),
            P(("fsdp", "seq"), None),
            P("fsdp", None),
            P("fsdp", None),
            P(),
            P(("fsdp", "seq"), None),
        ),
        out_specs=(
            P(("fsdp", "seq"), None),
            P(("fsdp", "seq"), None),
            P(("fsdp", "seq"), None),
            P(("fsdp", "seq"), None),
            P(("fsdp", "seq"), None),
            P("fsdp", None),
            P("fsdp", None),
        ),
        check_vma=False,
    )
```

profile of v0, /device:TPU:0, one launch (start us, length us, event | category | flops | bytes accessed | tf_op | source)
XLA Modules:
  0.0 841.6 jit_solution(16529460846051398073)
XLA Ops:
  7.2 3.7 collective-permute-start
  11.0 3.5 collective-permute-start.16
  17.1 5.2 collective-permute-start.1
  23.8 3.9 collective-permute-start.34
  28.4 3.2 collective-permute-start.17
  34.2 6.9 collective-permute-start.2
  41.1 3.9 collective-permute-start.18
  47.7 5.2 collective-permute-start.3
  54.7 16.8 %all_gather.7 = bf16[32,1536]{1,0:T(8,128)(2,1)S(1)} all-gather(bf16[8,1536]{1,0:T(8,128)(2,1)} %param.13), channel_id=1, replica_groups=mesh['fsdp'=4,'seq'=32] {'fsdp'}, dimensions={0}, use_global_device_ids=true | all-gather | bytes 122880 | tf_op jit(solution)/shard_map/all_gather | solution.py:70
  77.3 5.9 collective-permute-start.4
  84.1 3.9 collective-permute-start.20
  90.6 5.9 collective-permute-start.5
  99.6 4.6 collective-permute-start.21
  106.7 5.2 collective-permute-start.6
  113.1 4.6 collective-permute-start.22
  120.3 5.5 collective-permute-start.7
  125.8 4.2 fusion.14
  130.4 6.8 collective-permute-start.23
  143.9 5.3 collective-permute-done.15
  150.7 3.9 copy.43
  171.5 4.1 copy.48
  183.6 3.2 convolution_convert_fusion.2
  191.3 5.0 fusion.141
  196.3 3.0 fusion.6
  199.3 3.5 copy.69
  202.9 6.3 fusion.144
  209.2 5.3 fusion.7
  214.4 5.2 copy.68
  225.3 5.1 copy.64
  230.5 4.2 convolution_multiply_fusion.2
  234.7 5.1 copy.65
  245.2 6.9 collective-permute-done.36
  258.4 2.9 fusion.147
  269.6 14.1 %collective-permute-done.38 = f32[128,768]{1,0:T(8,128)S(1)} collective-permute-done((f32[128,768]{1,0:T(8,128)S(1)}, f32[128,768]{1,0:T(8,128)S(1)}, u32[]{:S(2)}, u32[]{:S(2)}) %collective-permute-start.38) | collective-permute-done | bytes 393248 | tf_op jit(solution)/shard_map/ppermute | solution.py:18
  285.0 7.1 collective-permute-done.55
  293.4 8.3 collective-permute-done.39
  303.1 7.1 collective-permute-done.56
  311.5 7.1 collective-permute-done.40
  319.9 7.1 collective-permute-done.57
  328.3 7.1 collective-permute-done.41
  336.8 7.1 collective-permute-done.58
  344.7 7.1 collective-permute-start.60
  353.1 6.8 collective-permute-start.44
  361.5 5.2 collective-permute-start.61
  367.1 5.9 collective-permute-start.45
  376.2 5.5 collective-permute-start.62
  381.7 2.8 collective-permute-done.45
  384.6 5.3 collective-permute-start.46
  393.8 6.3 collective-permute-start.63
  402.2 6.0 collective-permute-start.47
  409.5 6.5 collective-permute-start.32
  420.4 5.9 collective-permute-start.64
  427.4 6.5 collective-permute-start.48
  435.0 5.9 collective-permute-start.65
  442.9 6.3 collective-permute-start.49
  451.5 7.1 collective-permute-start.66
  459.8 6.4 collective-permute-start.50
  467.9 2.8 stack.131
  475.3 9.0 %collective-permute-start.67 = (f32[128,768]{1,0:T(8,128)S(1)}, f32[128,768]{1,0:T(8,128)}, u32[]{:S(2)}, u32[]{:S(2)}) collective-permute-start(f32[128,768]{1,0:T(8,128)S(1)} %fusion.139), channel_id=1, source_target_pairs={{0,1},{1,2},{2,3},{3,4},{4,5},{5,6},{6,7},{7,8},{8,9},{9,10},{10,1... | collective-permute-start | bytes 1179656 | tf_op jit(solution)/shard_map/ppermute | solution.py:18
  484.4 5.6 collective-permute-start.51
  490.3 4.7 add_convert_fusion
  494.9 29.9 %reduce-scatter.5.cloned.1.call-done = f32[8,1536]{1,0:T(8,128)} async-done(((f32[32,1536]{1,0:T(8,128)}), f32[8,1536]{1,0:T(8,128)}) %reduce-scatter.5.cloned.1.call-update) | async-done | bytes 49168 | tf_op jit(solution)/shard_map/reduce_scatter | solution.py:133
  524.9 157.0 %psum.17 = f32[8,1536]{1,0:T(8,128)} all-reduce(f32[8,1536]{1,0:T(8,128)} %reduce-scatter.5.cloned.1.call-done), channel_id=1, replica_groups=mesh['fsdp'=4,'seq'=32] {'seq'}, use_global_device_ids=true, to_apply=%region_39.40 | all-reduce | flops 12288 | bytes 98304 | tf_op jit(solution)/shard_map/psum | solution.py:130
  687.0 145.3 %all-reduce.2.cloned.1.call-done = f32[192,1536]{1,0:T(8,128)} async-done(((f32[192,1536]{1,0:T(8,128)}), f32[192,1536]{1,0:T(8,128)}) %all-reduce.2.cloned.1.call-update) | async-done | bytes 1179664 | tf_op jit(solution)/shard_map/psum | solution.py:130
  (477 shorter events, 141.7 us)
Async XLA Ops:
  7.2 179.9 %all-gather.2.cloned.1.call-start = ((), (), s32[]{:S(2)}) async-start(), calls=%async_computation.2 | async-start | bytes 2949120 | tf_op jit(solution)/shard_map/all_gather | solution.py:69
  11.0 17.4 %collective-permute-start.16 = (bf16[128,768]{1,0:T(8,128)(2,1)}, bf16[128,768]{1,0:T(8,128)(2,1)S(1)}, u32[]{:S(2)}, u32[]{:S(2)}) collective-permute-start(bf16[128,768]{1,0:T(8,128)(2,1)} %param.10), channel_id=1, source_target_pairs={{0,1},{1,2},{2,3},{3,4},{4,5},{5,6},{6,7},{7,8},{8,9},{9,10},{10,1... | collective-permute-start | bytes 589832 | tf_op jit(solution)/shard_map/ppermute | solution.py:18
  14.5 17.1 %collective-permute-start.24 = (bf16[128,768]{1,0:T(8,128)(2,1)}, bf16[128,768]{1,0:T(8,128)(2,1)S(1)}, u32[]{:S(2)}, u32[]{:S(2)}) collective-permute-start(bf16[128,768]{1,0:T(8,128)(2,1)} %param.10), channel_id=1, source_target_pairs={{1,0},{2,1},{3,2},{4,3},{5,4},{6,5},{7,6},{8,7},{9,8},{10,9},{11,1... | collective-permute-start | bytes 589832 | tf_op jit(solution)/shard_map/ppermute | solution.py:18
  15.8 17.1 %collective-permute-start.8 = (bf16[128,768]{1,0:T(8,128)(2,1)}, bf16[128,768]{1,0:T(8,128)(2,1)S(1)}, u32[]{:S(2)}, u32[]{:S(2)}) collective-permute-start(bf16[128,768]{1,0:T(8,128)(2,1)} %param.11), channel_id=1, source_target_pairs={{1,0},{2,1},{3,2},{4,3},{5,4},{6,5},{7,6},{8,7},{9,8},{10,9},{11,1... | collective-permute-start | bytes 589832 | tf_op jit(solution)/shard_map/ppermute | solution.py:18
  17.1 472.9 %reduce-scatter.3.cloned.1.call-start = ((), (), s32[]{:S(2)}) async-start(), calls=%async_computation.3 | async-start | bytes 5898240 | tf_op jit(solution)/shard_map/reduce_scatter | solution.py:132
  17.1 17.1 %collective-permute-start.1 = (bf16[128,768]{1,0:T(8,128)(2,1)S(1)}, bf16[128,768]{1,0:T(8,128)(2,1)S(1)}, u32[]{:S(2)}, u32[]{:S(2)}) collective-permute-start(bf16[128,768]{1,0:T(8,128)(2,1)S(1)} %collective-permute-done), channel_id=1, source_target_pairs={{0,1},{1,2},{2,3},{3,4},{4,5},{5,6},{6,7},{7,8},{8,9},{9,10},{10,1... | collective-permute-start | bytes 589832 | tf_op jit(solution)/shard_map/ppermute | solution.py:18
  23.8 73.6 %collective-permute-start.34 = (bf16[16,1536]{1,0:T(8,128)(2,1)S(1)}, bf16[16,1536]{1,0:T(8,128)(2,1)S(1)}, u32[]{:S(2)}, u32[]{:S(2)}) collective-permute-start(bf16[16,1536]{1,0:T(8,128)(2,1)S(1)} %get-tuple-element.81), channel_id=1, source_target_pairs={{0,1},{1,2},{2,3},{3,4},{4,5},{5,6},{6,7},{7,8},{8,9},{9,10},{10,1... | collective-permute-start | bytes 147464 | tf_op jit(solution)/shard_map/ppermute | solution.py:26
  31.6 13.5 %collective-permute-start.25 = (bf16[128,768]{1,0:T(8,128)(2,1)S(1)}, bf16[128,768]{1,0:T(8,128)(2,1)S(1)}, u32[]{:S(2)}, u32[]{:S(2)}) collective-permute-start(bf16[128,768]{1,0:T(8,128)(2,1)S(1)} %collective-permute-done.24), channel_id=1, source_target_pairs={{1,0},{2,1},{3,2},{4,3},{5,4},{6,5},{7,6},{8,7},{9,8},{10,9},{11,1... | collective-permute-start | bytes 589832 | tf_op jit(solution)/shard_map/ppermute | solution.py:18
  32.9 13.5 %collective-permute-start.9 = (bf16[128,768]{1,0:T(8,128)(2,1)S(1)}, bf16[128,768]{1,0:T(8,128)(2,1)S(1)}, u32[]{:S(2)}, u32[]{:S(2)}) collective-permute-start(bf16[128,768]{1,0:T(8,128)(2,1)S(1)} %collective-permute-done.8), channel_id=1, source_target_pairs={{1,0},{2,1},{3,2},{4,3},{5,4},{6,5},{7,6},{8,7},{9,8},{10,9},{11,1... | collective-permute-start | bytes 589832 | tf_op jit(solution)/shard_map/ppermute | solution.py:18
  34.2 13.5 %collective-permute-start.2 = (bf16[128,768]{1,0:T(8,128)(2,1)S(1)}, bf16[128,768]{1,0:T(8,128)(2,1)S(1)}, u32[]{:S(2)}, u32[]{:S(2)}) collective-permute-start(bf16[128,768]{1,0:T(8,128)(2,1)S(1)} %collective-permute-done.1), channel_id=1, source_target_pairs={{0,1},{1,2},{2,3},{3,4},{4,5},{5,6},{6,7},{7,8},{8,9},{9,10},{10,1... | collective-permute-start | bytes 589832 | tf_op jit(solution)/shard_map/ppermute | solution.py:18
  41.1 30.9 %collective-permute-start.18 = (bf16[128,768]{1,0:T(8,128)(2,1)S(1)}, bf16[128,768]{1,0:T(8,128)(2,1)S(1)}, u32[]{:S(2)}, u32[]{:S(2)}) collective-permute-start(bf16[128,768]{1,0:T(8,128)(2,1)S(1)} %collective-permute-done.17), channel_id=1, source_target_pairs={{0,1},{1,2},{2,3},{3,4},{4,5},{5,6},{6,7},{7,8},{8,9},{9,10},{10,1... | collective-permute-start | bytes 589832 | tf_op jit(solution)/shard_map/ppermute | solution.py:18
  45.1 29.5 %collective-permute-start.26 = (bf16[128,768]{1,0:T(8,128)(2,1)S(1)}, bf16[128,768]{1,0:T(8,128)(2,1)S(1)}, u32[]{:S(2)}, u32[]{:S(2)}) collective-permute-start(bf16[128,768]{1,0:T(8,128)(2,1)S(1)} %collective-permute-done.25), channel_id=1, source_target_pairs={{1,0},{2,1},{3,2},{4,3},{5,4},{6,5},{7,6},{8,7},{9,8},{10,9},{11,1... | collective-permute-start | bytes 589832 | tf_op jit(solution)/shard_map/ppermute | solution.py:18
  46.4 29.5 %collective-permute-start.10 = (bf16[128,768]{1,0:T(8,128)(2,1)S(1)}, bf16[128,768]{1,0:T(8,128)(2,1)S(1)}, u32[]{:S(2)}, u32[]{:S(2)}) collective-permute-start(bf16[128,768]{1,0:T(8,128)(2,1)S(1)} %collective-permute-done.9), channel_id=1, source_target_pairs={{1,0},{2,1},{3,2},{4,3},{5,4},{6,5},{7,6},{8,7},{9,8},{10,9},{11,1... | collective-permute-start | bytes 589832 | tf_op jit(solution)/shard_map/ppermute | solution.py:18
  47.7 29.5 %collective-permute-start.3 = (bf16[128,768]{1,0:T(8,128)(2,1)S(1)}, bf16[128,768]{1,0:T(8,128)(2,1)S(1)}, u32[]{:S(2)}, u32[]{:S(2)}) collective-permute-start(bf16[128,768]{1,0:T(8,128)(2,1)S(1)} %collective-permute-done.2), channel_id=1, source_target_pairs={{0,1},{1,2},{2,3},{3,4},{4,5},{5,6},{6,7},{7,8},{8,9},{9,10},{10,1... | collective-permute-start | bytes 589832 | tf_op jit(solution)/shard_map/ppermute | solution.py:18
  74.6 13.4 %collective-permute-start.27 = (bf16[128,768]{1,0:T(8,128)(2,1)S(1)}, bf16[128,768]{1,0:T(8,128)(2,1)S(1)}, u32[]{:S(2)}, u32[]{:S(2)}) collective-permute-start(bf16[128,768]{1,0:T(8,128)(2,1)S(1)} %collective-permute-done.26), channel_id=1, source_target_pairs={{1,0},{2,1},{3,2},{4,3},{5,4},{6,5},{7,6},{8,7},{9,8},{10,9},{11,1... | collective-permute-start | bytes 589832 | tf_op jit(solution)/shard_map/ppermute | solution.py:18
  75.9 13.4 %collective-permute-start.11 = (bf16[128,768]{1,0:T(8,128)(2,1)S(1)}, bf16[128,768]{1,0:T(8,128)(2,1)}, u32[]{:S(2)}, u32[]{:S(2)}) collective-permute-start(bf16[128,768]{1,0:T(8,128)(2,1)S(1)} %collective-permute-done.10), channel_id=1, source_target_pairs={{1,0},{2,1},{3,2},{4,3},{5,4},{6,5},{7,6},{8,7},{9,8},{10,9},{11,1... | collective-permute-start | bytes 589832 | tf_op jit(solution)/shard_map/ppermute | solution.py:18
  77.3 13.4 %collective-permute-start.4 = (bf16[128,768]{1,0:T(8,128)(2,1)S(1)}, bf16[128,768]{1,0:T(8,128)(2,1)}, u32[]{:S(2)}, u32[]{:S(2)}) collective-permute-start(bf16[128,768]{1,0:T(8,128)(2,1)S(1)} %collective-permute-done.3), channel_id=1, source_target_pairs={{0,1},{1,2},{2,3},{3,4},{4,5},{5,6},{6,7},{7,8},{8,9},{9,10},{10,1... | collective-permute-start | bytes 589832 | tf_op jit(solution)/shard_map/ppermute | solution.py:18
  84.1 15.5 %collective-permute-start.20 = (bf16[128,768]{1,0:T(8,128)(2,1)}, bf16[128,768]{1,0:T(8,128)(2,1)}, u32[]{:S(2)}, u32[]{:S(2)}) collective-permute-start(bf16[128,768]{1,0:T(8,128)(2,1)} %collective-permute-done.19), channel_id=1, source_target_pairs={{0,1},{1,2},{2,3},{3,4},{4,5},{5,6},{6,7},{7,8},{8,9},{9,10},{10,1... | collective-permute-start | bytes 589832 | tf_op jit(solution)/shard_map/ppermute | solution.py:18
  88.0 16.1 %collective-permute-start.28 = (bf16[128,768]{1,0:T(8,128)(2,1)S(1)}, bf16[128,768]{1,0:T(8,128)(2,1)}, u32[]{:S(2)}, u32[]{:S(2)}) collective-permute-start(bf16[128,768]{1,0:T(8,128)(2,1)S(1)} %collective-permute-done.27), channel_id=1, source_target_pairs={{1,0},{2,1},{3,2},{4,3},{5,4},{6,5},{7,6},{8,7},{9,8},{10,9},{11,1... | collective-permute-start | bytes 589832 | tf_op jit(solution)/shard_map/ppermute | solution.py:18
  89.3 16.1 %collective-permute-start.12 = (bf16[128,768]{1,0:T(8,128)(2,1)}, bf16[128,768]{1,0:T(8,128)(2,1)}, u32[]{:S(2)}, u32[]{:S(2)}) collective-permute-start(bf16[128,768]{1,0:T(8,128)(2,1)} %collective-permute-done.11), channel_id=1, source_target_pairs={{1,0},{2,1},{3,2},{4,3},{5,4},{6,5},{7,6},{8,7},{9,8},{10,9},{11,1... | collective-permute-start | bytes 589832 | tf_op jit(solution)/shard_map/ppermute | solution.py:18
  90.6 16.1 %collective-permute-start.5 = (bf16[128,768]{1,0:T(8,128)(2,1)}, bf16[128,768]{1,0:T(8,128)(2,1)}, u32[]{:S(2)}, u32[]{:S(2)}) collective-permute-start(bf16[128,768]{1,0:T(8,128)(2,1)} %collective-permute-done.4), channel_id=1, source_target_pairs={{0,1},{1,2},{2,3},{3,4},{4,5},{5,6},{6,7},{7,8},{8,9},{9,10},{10,1... | collective-permute-start | bytes 589832 | tf_op jit(solution)/shard_map/ppermute | solution.py:18
  97.4 14.6 %collective-permute-start.35 = (bf16[16,1536]{1,0:T(8,128)(2,1)}, bf16[16,1536]{1,0:T(8,128)(2,1)S(1)}, u32[]{:S(2)}, u32[]{:S(2)}) collective-permute-start(bf16[16,1536]{1,0:T(8,128)(2,1)} %get-tuple-element.82), channel_id=1, source_target_pairs={{1,0},{2,1},{3,2},{4,3},{5,4},{6,5},{7,6},{8,7},{9,8},{10,9},{11,1... | collective-permute-start | bytes 147464 | tf_op jit(solution)/shard_map/ppermute | solution.py:29
  99.6 13.5 %collective-permute-start.21 = (bf16[128,768]{1,0:T(8,128)(2,1)}, bf16[128,768]{1,0:T(8,128)(2,1)S(1)}, u32[]{:S(2)}, u32[]{:S(2)}) collective-permute-start(bf16[128,768]{1,0:T(8,128)(2,1)} %collective-permute-done.20), channel_id=1, source_target_pairs={{0,1},{1,2},{2,3},{3,4},{4,5},{5,6},{6,7},{7,8},{8,9},{9,10},{10,1... | collective-permute-start | bytes 589832 | tf_op jit(solution)/shard_map/ppermute | solution.py:18
  104.1 13.5 %collective-permute-start.29 = (bf16[128,768]{1,0:T(8,128)(2,1)}, bf16[128,768]{1,0:T(8,128)(2,1)S(1)}, u32[]{:S(2)}, u32[]{:S(2)}) collective-permute-start(bf16[128,768]{1,0:T(8,128)(2,1)} %collective-permute-done.28), channel_id=1, source_target_pairs={{1,0},{2,1},{3,2},{4,3},{5,4},{6,5},{7,6},{8,7},{9,8},{10,9},{11,1... | collective-permute-start | bytes 589832 | tf_op jit(solution)/shard_map/ppermute | solution.py:18
  105.4 13.5 %collective-permute-start.13 = (bf16[128,768]{1,0:T(8,128)(2,1)}, bf16[128,768]{1,0:T(8,128)(2,1)S(1)}, u32[]{:S(2)}, u32[]{:S(2)}) collective-permute-start(bf16[128,768]{1,0:T(8,128)(2,1)} %collective-permute-done.12), channel_id=1, source_target_pairs={{1,0},{2,1},{3,2},{4,3},{5,4},{6,5},{7,6},{8,7},{9,8},{10,9},{11,1... | collective-permute-start | bytes 589832 | tf_op jit(solution)/shard_map/ppermute | solution.py:18
  106.7 13.5 %collective-permute-start.6 = (bf16[128,768]{1,0:T(8,128)(2,1)}, bf16[128,768]{1,0:T(8,128)(2,1)S(1)}, u32[]{:S(2)}, u32[]{:S(2)}) collective-permute-start(bf16[128,768]{1,0:T(8,128)(2,1)} %collective-permute-done.5), channel_id=1, source_target_pairs={{0,1},{1,2},{2,3},{3,4},{4,5},{5,6},{6,7},{7,8},{8,9},{9,10},{10,1... | collective-permute-start | bytes 589832 | tf_op jit(solution)/shard_map/ppermute | solution.py:18
  113.1 17.3 %collective-permute-start.22 = (bf16[128,768]{1,0:T(8,128)(2,1)S(1)}, bf16[128,768]{1,0:T(8,128)(2,1)}, u32[]{:S(2)}, u32[]{:S(2)}) collective-permute-start(bf16[128,768]{1,0:T(8,128)(2,1)S(1)} %collective-permute-done.21), channel_id=1, source_target_pairs={{0,1},{1,2},{2,3},{3,4},{4,5},{5,6},{6,7},{7,8},{8,9},{9,10},{10,1... | collective-permute-start | bytes 589832 | tf_op jit(solution)/shard_map/ppermute | solution.py:18
  117.7 19.6 %collective-permute-start.30 = (bf16[128,768]{1,0:T(8,128)(2,1)S(1)}, bf16[128,768]{1,0:T(8,128)(2,1)}, u32[]{:S(2)}, u32[]{:S(2)}) collective-permute-start(bf16[128,768]{1,0:T(8,128)(2,1)S(1)} %collective-permute-done.29), channel_id=1, source_target_pairs={{1,0},{2,1},{3,2},{4,3},{5,4},{6,5},{7,6},{8,7},{9,8},{10,9},{11,1... | collective-permute-start | bytes 589832 | tf_op jit(solution)/shard_map/ppermute | solution.py:18
  119.0 19.5 %collective-permute-start.14 = (bf16[128,768]{1,0:T(8,128)(2,1)S(1)}, bf16[128,768]{1,0:T(8,128)(2,1)S(1)}, u32[]{:S(2)}, u32[]{:S(2)}) collective-permute-start(bf16[128,768]{1,0:T(8,128)(2,1)S(1)} %collective-permute-done.13), channel_id=1, source_target_pairs={{1,0},{2,1},{3,2},{4,3},{5,4},{6,5},{7,6},{8,7},{9,8},{10,9},{11,1... | collective-permute-start | bytes 589832 | tf_op jit(solution)/shard_map/ppermute | solution.py:18
  120.3 19.5 %collective-permute-start.7 = (bf16[128,768]{1,0:T(8,128)(2,1)S(1)}, bf16[128,768]{1,0:T(8,128)(2,1)S(1)}, u32[]{:S(2)}, u32[]{:S(2)}) collective-permute-start(bf16[128,768]{1,0:T(8,128)(2,1)S(1)} %collective-permute-done.6), channel_id=1, source_target_pairs={{0,1},{1,2},{2,3},{3,4},{4,5},{5,6},{6,7},{7,8},{8,9},{9,10},{10,1... | collective-permute-start | bytes 589832 | tf_op jit(solution)/shard_map/ppermute | solution.py:18
  130.4 26.6 %collective-permute-start.23 = (bf16[128,768]{1,0:T(8,128)(2,1)}, bf16[128,768]{1,0:T(8,128)(2,1)}, u32[]{:S(2)}, u32[]{:S(2)}) collective-permute-start(bf16[128,768]{1,0:T(8,128)(2,1)} %collective-permute-done.22), channel_id=1, source_target_pairs={{0,1},{1,2},{2,3},{3,4},{4,5},{5,6},{6,7},{7,8},{8,9},{9,10},{10,1... | collective-permute-start | bytes 589832 | tf_op jit(solution)/shard_map/ppermute | solution.py:18
  137.2 28.6 %collective-permute-start.31 = (bf16[128,768]{1,0:T(8,128)(2,1)}, bf16[128,768]{1,0:T(8,128)(2,1)}, u32[]{:S(2)}, u32[]{:S(2)}) collective-permute-start(bf16[128,768]{1,0:T(8,128)(2,1)} %collective-permute-done.30), channel_id=1, source_target_pairs={{1,0},{2,1},{3,2},{4,3},{5,4},{6,5},{7,6},{8,7},{9,8},{10,9},{11,1... | collective-permute-start | bytes 589832 | tf_op jit(solution)/shard_map/ppermute | solution.py:18
  221.5 21.1 %collective-permute-start.52 = (f32[128,768]{1,0:T(8,128)}, f32[128,768]{1,0:T(8,128)}, u32[]{:S(2)}, u32[]{:S(2)}) collective-permute-start(f32[128,768]{1,0:T(8,128)} %fusion.81), channel_id=1, source_target_pairs={{1,0},{2,1},{3,2},{4,3},{5,4},{6,5},{7,6},{8,7},{9,8},{10,9},{11,1... | collective-permute-start | bytes 1179656 | tf_op jit(solution)/shard_map/ppermute | solution.py:18
  261.4 263.5 %reduce-scatter.5.cloned.1.call-start = ((), (), s32[]{:S(2)}) async-start(), calls=%async_computation.5 | async-start | bytes 245760 | tf_op jit(solution)/shard_map/reduce_scatter | solution.py:133
  264.2 19.4 %collective-permute-start.38 = (f32[128,768]{1,0:T(8,128)S(1)}, f32[128,768]{1,0:T(8,128)S(1)}, u32[]{:S(2)}, u32[]{:S(2)}) collective-permute-start(f32[128,768]{1,0:T(8,128)S(1)} %fusion.121), channel_id=1, source_target_pairs={{1,0},{2,1},{3,2},{4,3},{5,4},{6,5},{7,6},{8,7},{9,8},{10,9},{11,1... | collective-permute-start | bytes 1179656 | tf_op jit(solution)/shard_map/ppermute | solution.py:18
  268.3 23.8 %collective-permute-start.55 = (f32[128,768]{1,0:T(8,128)S(1)}, f32[128,768]{1,0:T(8,128)S(1)}, u32[]{:S(2)}, u32[]{:S(2)}) collective-permute-start(f32[128,768]{1,0:T(8,128)S(1)} %fusion.134), channel_id=1, source_target_pairs={{1,0},{2,1},{3,2},{4,3},{5,4},{6,5},{7,6},{8,7},{9,8},{10,9},{11,1... | collective-permute-start | bytes 1179656 | tf_op jit(solution)/shard_map/ppermute | solution.py:18
  283.7 18.0 %collective-permute-start.39 = (f32[128,768]{1,0:T(8,128)S(1)}, f32[128,768]{1,0:T(8,128)S(1)}, u32[]{:S(2)}, u32[]{:S(2)}) collective-permute-start(f32[128,768]{1,0:T(8,128)S(1)} %fusion.120), channel_id=1, source_target_pairs={{1,0},{2,1},{3,2},{4,3},{5,4},{6,5},{7,6},{8,7},{9,8},{10,9},{11,1... | collective-permute-start | bytes 1179656 | tf_op jit(solution)/shard_map/ppermute | solution.py:18
  292.1 18.0 %collective-permute-start.56 = (f32[128,768]{1,0:T(8,128)S(1)}, f32[128,768]{1,0:T(8,128)S(1)}, u32[]{:S(2)}, u32[]{:S(2)}) collective-permute-start(f32[128,768]{1,0:T(8,128)S(1)} %fusion.133), channel_id=1, source_target_pairs={{1,0},{2,1},{3,2},{4,3},{5,4},{6,5},{7,6},{8,7},{9,8},{10,9},{11,1... | collective-permute-start | bytes 1179656 | tf_op jit(solution)/shard_map/ppermute | solution.py:18
  301.8 16.8 %collective-permute-start.40 = (f32[128,768]{1,0:T(8,128)S(1)}, f32[128,768]{1,0:T(8,128)S(1)}, u32[]{:S(2)}, u32[]{:S(2)}) collective-permute-start(f32[128,768]{1,0:T(8,128)S(1)} %fusion.119), channel_id=1, source_target_pairs={{1,0},{2,1},{3,2},{4,3},{5,4},{6,5},{7,6},{8,7},{9,8},{10,9},{11,1... | collective-permute-start | bytes 1179656 | tf_op jit(solution)/shard_map/ppermute | solution.py:18
  310.2 16.8 %collective-permute-start.57 = (f32[128,768]{1,0:T(8,128)S(1)}, f32[128,768]{1,0:T(8,128)S(1)}, u32[]{:S(2)}, u32[]{:S(2)}) collective-permute-start(f32[128,768]{1,0:T(8,128)S(1)} %fusion.132), channel_id=1, source_target_pairs={{1,0},{2,1},{3,2},{4,3},{5,4},{6,5},{7,6},{8,7},{9,8},{10,9},{11,1... | collective-permute-start | bytes 1179656 | tf_op jit(solution)/shard_map/ppermute | solution.py:18
  318.6 16.8 %collective-permute-start.41 = (f32[128,768]{1,0:T(8,128)S(1)}, f32[128,768]{1,0:T(8,128)S(1)}, u32[]{:S(2)}, u32[]{:S(2)}) collective-permute-start(f32[128,768]{1,0:T(8,128)S(1)} %fusion.118), channel_id=1, source_target_pairs={{1,0},{2,1},{3,2},{4,3},{5,4},{6,5},{7,6},{8,7},{9,8},{10,9},{11,1... | collective-permute-start | bytes 1179656 | tf_op jit(solution)/shard_map/ppermute | solution.py:18
  327.0 16.8 %collective-permute-start.58 = (f32[128,768]{1,0:T(8,128)S(1)}, f32[128,768]{1,0:T(8,128)S(1)}, u32[]{:S(2)}, u32[]{:S(2)}) collective-permute-start(f32[128,768]{1,0:T(8,128)S(1)} %fusion.131), channel_id=1, source_target_pairs={{1,0},{2,1},{3,2},{4,3},{5,4},{6,5},{7,6},{8,7},{9,8},{10,9},{11,1... | collective-permute-start | bytes 1179656 | tf_op jit(solution)/shard_map/ppermute | solution.py:18
  335.5 16.8 %collective-permute-start.42 = (f32[128,768]{1,0:T(8,128)S(1)}, f32[128,768]{1,0:T(8,128)S(1)}, u32[]{:S(2)}, u32[]{:S(2)}) collective-permute-start(f32[128,768]{1,0:T(8,128)S(1)} %fusion.117), channel_id=1, source_target_pairs={{1,0},{2,1},{3,2},{4,3},{5,4},{6,5},{7,6},{8,7},{9,8},{10,9},{11,1... | collective-permute-start | bytes 1179656 | tf_op jit(solution)/shard_map/ppermute | solution.py:18
  344.7 16.7 %collective-permute-start.60 = (f32[128,768]{1,0:T(8,128)S(1)}, f32[128,768]{1,0:T(8,128)S(1)}, u32[]{:S(2)}, u32[]{:S(2)}) collective-permute-start(f32[128,768]{1,0:T(8,128)S(1)} %get-tuple-element.74), channel_id=1, source_target_pairs={{0,1},{1,2},{2,3},{3,4},{4,5},{5,6},{6,7},{7,8},{8,9},{9,10},{10,1... | collective-permute-start | bytes 1179656 | tf_op jit(solution)/shard_map/ppermute | solution.py:18
  353.1 13.9 %collective-permute-start.44 = (f32[128,768]{1,0:T(8,128)S(1)}, f32[128,768]{1,0:T(8,128)S(1)}, u32[]{:S(2)}, u32[]{:S(2)}) collective-permute-start(f32[128,768]{1,0:T(8,128)S(1)} %get-tuple-element.76), channel_id=1, source_target_pairs={{0,1},{1,2},{2,3},{3,4},{4,5},{5,6},{6,7},{7,8},{8,9},{9,10},{10,1... | collective-permute-start | bytes 1179656 | tf_op jit(solution)/shard_map/ppermute | solution.py:18
  361.5 14.7 %collective-permute-start.61 = (f32[128,768]{1,0:T(8,128)S(1)}, f32[128,768]{1,0:T(8,128)S(1)}, u32[]{:S(2)}, u32[]{:S(2)}) collective-permute-start(f32[128,768]{1,0:T(8,128)S(1)} %fusion.129), channel_id=1, source_target_pairs={{0,1},{1,2},{2,3},{3,4},{4,5},{5,6},{6,7},{7,8},{8,9},{9,10},{10,1... | collective-permute-start | bytes 1179656 | tf_op jit(solution)/shard_map/ppermute | solution.py:18
  367.1 17.5 %collective-permute-start.45 = (f32[128,768]{1,0:T(8,128)S(1)}, f32[128,768]{1,0:T(8,128)S(1)}, u32[]{:S(2)}, u32[]{:S(2)}) collective-permute-start(f32[128,768]{1,0:T(8,128)S(1)} %fusion.115), channel_id=1, source_target_pairs={{0,1},{1,2},{2,3},{3,4},{4,5},{5,6},{6,7},{7,8},{8,9},{9,10},{10,1... | collective-permute-start | bytes 1179656 | tf_op jit(solution)/shard_map/ppermute | solution.py:18
  376.2 16.8 %collective-permute-start.62 = (f32[128,768]{1,0:T(8,128)S(1)}, f32[128,768]{1,0:T(8,128)S(1)}, u32[]{:S(2)}, u32[]{:S(2)}) collective-permute-start(f32[128,768]{1,0:T(8,128)S(1)} %fusion.128), channel_id=1, source_target_pairs={{0,1},{1,2},{2,3},{3,4},{4,5},{5,6},{6,7},{7,8},{8,9},{9,10},{10,1... | collective-permute-start | bytes 1179656 | tf_op jit(solution)/shard_map/ppermute | solution.py:18
  384.6 16.8 %collective-permute-start.46 = (f32[128,768]{1,0:T(8,128)S(1)}, f32[128,768]{1,0:T(8,128)S(1)}, u32[]{:S(2)}, u32[]{:S(2)}) collective-permute-start(f32[128,768]{1,0:T(8,128)S(1)} %fusion.114), channel_id=1, source_target_pairs={{0,1},{1,2},{2,3},{3,4},{4,5},{5,6},{6,7},{7,8},{8,9},{9,10},{10,1... | collective-permute-start | bytes 1179656 | tf_op jit(solution)/shard_map/ppermute | solution.py:18
  393.8 25.3 %collective-permute-start.63 = (f32[128,768]{1,0:T(8,128)}, f32[128,768]{1,0:T(8,128)}, u32[]{:S(2)}, u32[]{:S(2)}) collective-permute-start(f32[128,768]{1,0:T(8,128)} %fusion.127), channel_id=1, source_target_pairs={{0,1},{1,2},{2,3},{3,4},{4,5},{5,6},{6,7},{7,8},{8,9},{9,10},{10,1... | collective-permute-start | bytes 1179656 | tf_op jit(solution)/shard_map/ppermute | solution.py:18
  402.2 24.1 %collective-permute-start.47 = (f32[128,768]{1,0:T(8,128)}, f32[128,768]{1,0:T(8,128)}, u32[]{:S(2)}, u32[]{:S(2)}) collective-permute-start(f32[128,768]{1,0:T(8,128)} %fusion.113), channel_id=1, source_target_pairs={{0,1},{1,2},{2,3},{3,4},{4,5},{5,6},{6,7},{7,8},{8,9},{9,10},{10,1... | collective-permute-start | bytes 1179656 | tf_op jit(solution)/shard_map/ppermute | solution.py:18
  409.5 24.4 %collective-permute-start.32 = (bf16[16,1536]{1,0:T(8,128)(2,1)}, bf16[16,1536]{1,0:T(8,128)(2,1)}, u32[]{:S(2)}, u32[]{:S(2)}) collective-permute-start(bf16[16,1536]{1,0:T(8,128)(2,1)} %get-tuple-element.83), channel_id=1, source_target_pairs={{0,1},{1,2},{2,3},{3,4},{4,5},{5,6},{6,7},{7,8},{8,9},{9,10},{10,1... | collective-permute-start | bytes 147464 | tf_op jit(solution)/shard_map/ppermute | solution.py:26
  416.0 17.9 %collective-permute-start.33 = (bf16[16,1536]{1,0:T(8,128)(2,1)}, bf16[16,1536]{1,0:T(8,128)(2,1)}, u32[]{:S(2)}, u32[]{:S(2)}) collective-permute-start(bf16[16,1536]{1,0:T(8,128)(2,1)} %get-tuple-element.84), channel_id=1, source_target_pairs={{1,0},{2,1},{3,2},{4,3},{5,4},{6,5},{7,6},{8,7},{9,8},{10,9},{11,1... | collective-permute-start | bytes 147464 | tf_op jit(solution)/shard_map/ppermute | solution.py:29
  420.4 14.5 %collective-permute-start.64 = (f32[128,768]{1,0:T(8,128)S(1)}, f32[128,768]{1,0:T(8,128)S(1)}, u32[]{:S(2)}, u32[]{:S(2)}) collective-permute-start(f32[128,768]{1,0:T(8,128)S(1)} %fusion.126), channel_id=1, source_target_pairs={{0,1},{1,2},{2,3},{3,4},{4,5},{5,6},{6,7},{7,8},{8,9},{9,10},{10,1... | collective-permute-start | bytes 1179656 | tf_op jit(solution)/shard_map/ppermute | solution.py:18
  427.4 15.5 %collective-permute-start.48 = (f32[128,768]{1,0:T(8,128)S(1)}, f32[128,768]{1,0:T(8,128)S(1)}, u32[]{:S(2)}, u32[]{:S(2)}) collective-permute-start(f32[128,768]{1,0:T(8,128)S(1)} %fusion.112), channel_id=1, source_target_pairs={{0,1},{1,2},{2,3},{3,4},{4,5},{5,6},{6,7},{7,8},{8,9},{9,10},{10,1... | collective-permute-start | bytes 1179656 | tf_op jit(solution)/shard_map/ppermute | solution.py:18
  435.0 16.5 %collective-permute-start.65 = (f32[128,768]{1,0:T(8,128)S(1)}, f32[128,768]{1,0:T(8,128)S(1)}, u32[]{:S(2)}, u32[]{:S(2)}) collective-permute-start(f32[128,768]{1,0:T(8,128)S(1)} %fusion.125), channel_id=1, source_target_pairs={{0,1},{1,2},{2,3},{3,4},{4,5},{5,6},{6,7},{7,8},{8,9},{9,10},{10,1... | collective-permute-start | bytes 1179656 | tf_op jit(solution)/shard_map/ppermute | solution.py:18
  442.9 16.8 %collective-permute-start.49 = (f32[128,768]{1,0:T(8,128)S(1)}, f32[128,768]{1,0:T(8,128)S(1)}, u32[]{:S(2)}, u32[]{:S(2)}) collective-permute-start(f32[128,768]{1,0:T(8,128)S(1)} %fusion.111), channel_id=1, source_target_pairs={{0,1},{1,2},{2,3},{3,4},{4,5},{5,6},{6,7},{7,8},{8,9},{9,10},{10,1... | collective-permute-start | bytes 1179656 | tf_op jit(solution)/shard_map/ppermute | solution.py:18
  451.5 22.2 %collective-permute-start.66 = (f32[128,768]{1,0:T(8,128)S(1)}, f32[128,768]{1,0:T(8,128)S(1)}, u32[]{:S(2)}, u32[]{:S(2)}) collective-permute-start(f32[128,768]{1,0:T(8,128)S(1)} %fusion.138), channel_id=1, source_target_pairs={{0,1},{1,2},{2,3},{3,4},{4,5},{5,6},{6,7},{7,8},{8,9},{9,10},{10,1... | collective-permute-start | bytes 1179656 | tf_op jit(solution)/shard_map/ppermute | solution.py:18
  459.8 24.5 %collective-permute-start.50 = (f32[128,768]{1,0:T(8,128)S(1)}, f32[128,768]{1,0:T(8,128)S(1)}, u32[]{:S(2)}, u32[]{:S(2)}) collective-permute-start(f32[128,768]{1,0:T(8,128)S(1)} %fusion.124), channel_id=1, source_target_pairs={{0,1},{1,2},{2,3},{3,4},{4,5},{5,6},{6,7},{7,8},{8,9},{9,10},{10,1... | collective-permute-start | bytes 1179656 | tf_op jit(solution)/shard_map/ppermute | solution.py:18
  470.7 361.6 %all-reduce.2.cloned.1.call-start = ((), (), s32[]{:S(2)}) async-start(), calls=%async_computation.4 | async-start | bytes 2359296 | tf_op jit(solution)/shard_map/psum | solution.py:130
  470.8 211.2 %collective-permute-start.59 = (f32[128,768]{1,0:T(8,128)}, f32[128,768]{1,0:T(8,128)}, u32[]{:S(2)}, u32[]{:S(2)}) collective-permute-start(f32[128,768]{1,0:T(8,128)} %get-tuple-element.73), channel_id=1, source_target_pairs={{1,0},{2,1},{3,2},{4,3},{5,4},{6,5},{7,6},{8,7},{9,8},{10,9},{11,1... | collective-permute-start | bytes 1179656 | tf_op jit(solution)/shard_map/ppermute | solution.py:18
  472.1 211.9 %collective-permute-start.43 = (f32[128,768]{1,0:T(8,128)S(1)}, f32[128,768]{1,0:T(8,128)}, u32[]{:S(2)}, u32[]{:S(2)}) collective-permute-start(f32[128,768]{1,0:T(8,128)S(1)} %copy-done.42), channel_id=1, source_target_pairs={{1,0},{2,1},{3,2},{4,3},{5,4},{6,5},{7,6},{8,7},{9,8},{10,9},{11,1... | collective-permute-start | bytes 1179656 | tf_op jit(solution)/shard_map/ppermute | solution.py:18
  475.3 206.6 %collective-permute-start.67 = (f32[128,768]{1,0:T(8,128)S(1)}, f32[128,768]{1,0:T(8,128)}, u32[]{:S(2)}, u32[]{:S(2)}) collective-permute-start(f32[128,768]{1,0:T(8,128)S(1)} %fusion.139), channel_id=1, source_target_pairs={{0,1},{1,2},{2,3},{3,4},{4,5},{5,6},{6,7},{7,8},{8,9},{9,10},{10,1... | collective-permute-start | bytes 1179656 | tf_op jit(solution)/shard_map/ppermute | solution.py:18
  484.4 199.6 %collective-permute-start.51 = (f32[128,768]{1,0:T(8,128)S(1)}, f32[128,768]{1,0:T(8,128)S(1)}, u32[]{:S(2)}, u32[]{:S(2)}) collective-permute-start(f32[128,768]{1,0:T(8,128)S(1)} %fusion.140), channel_id=1, source_target_pairs={{0,1},{1,2},{2,3},{3,4},{4,5},{5,6},{6,7},{7,8},{8,9},{9,10},{10,1... | collective-permute-start | bytes 1179656 | tf_op jit(solution)/shard_map/ppermute | solution.py:18
  (124 other events, 3245.5 us)
Sparse Core Ops, SparseCore 0:
  17.2 50.1 all-gather.1
  261.5 88.3 reduce-scatter.2
  470.8 53.9 reduce-scatter.4
  527.2 305.0 all-reduce.1
where the time goes:
time: 851 us; the launch traced here: 842 us
  waiting for transfers between devices  270 us (32%)
  starting transfers between devices  232 us (27%)
  blocking collectives  174 us (20%)
  local copies, waits for them, and re-layouts  64.8 us (8%)
  matrix products  43.3 us (5%)
  other arithmetic  39 us (5%)
  between operations  17.8 us (2%)
    ppermute x64, starting transfers between devices, shifted_2(): lax.ppermute(value, axis, [(source, source + steps) for source in range(i...  219 us
    psum x1, blocking collectives, per_device(): summed = lax.psum((term_weight, term_kernel), 'seq')  157 us
    psum x1, waiting for transfers between devices, per_device(): summed = lax.psum((term_weight, term_kernel), 'seq')  145 us
    ppermute x64, waiting for transfers between devices, shifted_2(): lax.ppermute(value, axis, [(source, source + steps) for source in range(i...  95.1 us
    reduce_scatter x1, waiting for transfers between devices, per_device(): lax.psum_scatter(summed[1], 'fsdp', scatter_dimension=0, tiled=True)  29.9 us
    unnamed x265, local copies, waits for them, and re-layouts  18 us
  transfers between devices with their start and end apart: 72, of which 23 were waited for; matrix products, arithmetic and copies ran while one was open for 13% of the time, Pallas kernels for 0%

commit v1 on v0

v1 whole, which is shorter than its diff:
```python
import jax
import jax.numpy as jnp
from jax import lax
from jax.experimental import pallas as pl
from jax.experimental.pallas import tpu as pltpu
from jax.sharding import Mesh, PartitionSpec as P

HEADS = 8
HEAD = 96
TAPS = 32
WIN = 1024
D = 1536
FR = 128
SLAB = 8
QB = 256
NKB = 9
NB = 12
NEG = -1e30
LOG2E = 1.4426950408889634
SCALE = HEAD ** -0.5
AX = ("zh", "c", "x", "zl", "y")
SEQ = ("x", "zl", "y")
SL = ("zl", "y")
BF = jnp.bfloat16
F32 = jnp.float32
VM = pl.BlockSpec(memory_space=pltpu.VMEM)
SM = pl.BlockSpec(memory_space=pltpu.SMEM)


def shift(value, steps):
    n = 128
    pairs = [(i, i + steps) for i in range(max(0, -steps), min(n, n - steps))]
    return lax.ppermute(value, AX, pairs)


def pack_kernel(q, k, v, out):
    for n, ref in enumerate((q, k, v)):
        turned = ref[...].T
        for h in range(HEADS):
            out[h, n * HEAD : (n + 1) * HEAD, :] = turned[h * HEAD : (h + 1) * HEAD, :]


def pack(q, k, v):
    return pl.pallas_call(
        pack_kernel,
        out_shape=jax.ShapeDtypeStruct((HEADS, 3 * HEAD, FR), BF),
        in_specs=[VM] * 3,
        out_specs=VM,
        name="pack",
    )(q, k, v)


def attn_kernel(
    bounds, own, lo, hi, do, ctx_o, dq_o, dlo_o, down_o, dhi_o, kt, vt, ka, vn, s, e, dkt, dvt
):
    step = pl.program_id(0)

    @pl.when(step == 0)
    def _():
        first, last = bounds[0], bounds[1]
        pad_rows = lax.broadcasted_iota(jnp.int32, (32, FR), 0)
        lanes = lax.broadcasted_iota(jnp.int32, (32, FR), 1)
        for b in range(24):
            if b < 8:
                kb, vb = lo[b, 0:HEAD, :], lo[b, HEAD : 2 * HEAD, :]
            elif b < 16:
                kb, vb = own[b - 8, HEAD : 2 * HEAD, :], own[b - 8, 2 * HEAD : 3 * HEAD, :]
            else:
                kb, vb = hi[b - 16, 0:HEAD, :], hi[b - 16, HEAD : 2 * HEAD, :]
            pair, half = b // 2, b % 2
            cols = slice(half * FR, (half + 1) * FR)
            kt[pair, :, cols] = kb
            vt[pair, :, cols] = vb
            place = lanes + b * FR
            hidden = (pad_rows == 0) & ((place < first) | (place >= last))
            extra = jnp.where(hidden, NEG, 0.0).astype(BF)
            ka[pair, cols, :] = jnp.concatenate([kb, extra], axis=0).T
            vn[pair, cols, :] = jnp.concatenate([vb, jnp.zeros((32, FR), BF)], axis=0).T
        dkt[...] = jnp.zeros_like(dkt)
        dvt[...] = jnp.zeros_like(dvt)

    qt = jnp.concatenate([own[2 * step, 0:HEAD, :], own[2 * step + 1, 0:HEAD, :]], axis=1)
    ones = jnp.where(lax.broadcasted_iota(jnp.int32, (32, QB), 0) == 0, 1.0, 0.0).astype(BF)
    qa = jnp.concatenate([qt, ones], axis=0)
    kk = lax.broadcasted_iota(jnp.int32, (QB, QB), 0)
    qq = lax.broadcasted_iota(jnp.int32, (QB, QB), 1)
    top = None
    for r in range(NKB):
        part = jnp.dot(ka[step + r], qa, preferred_element_type=F32)
        if r == 0:
            part = jnp.where(kk >= qq, part, NEG)
        if r == NKB - 1:
            part = jnp.where(kk <= qq, part, NEG)
        s[r] = part
        peak = jnp.max(part, axis=0, keepdims=True)
        top = peak if top is None else jnp.maximum(top, peak)
    shift_top = top * (SCALE * LOG2E)
    total = jnp.zeros((1, QB), F32)
    out_t = jnp.zeros((HEAD, QB), F32)
    for r in range(NKB):
        part = jnp.exp2(s[r] * (SCALE * LOG2E) - shift_top)
        total = total + jnp.sum(part, axis=0, keepdims=True)
        rounded = part.astype(BF)
        e[r] = rounded
        out_t = out_t + jnp.dot(vt[step + r], rounded, preferred_element_type=F32)
    inverse = 1.0 / total
    ctx = (out_t * inverse).astype(BF)
    ctx_o[0] = ctx[:, :FR]
    ctx_o[1] = ctx[:, FR:]
    dot_ = jnp.concatenate([do[2 * step], do[2 * step + 1]], axis=1).astype(F32)
    delta = jnp.sum(dot_ * ctx.astype(F32), axis=0, keepdims=True) * inverse
    dos = (dot_ * inverse).astype(BF)
    dosa = jnp.concatenate([dos, jnp.zeros((32, QB), BF)], axis=0)
    dq = jnp.zeros((HEAD, QB), F32)
    nt = (((1,), (1,)), ((), ()))
    for r in range(NKB):
        dp = jnp.dot(vn[step + r], dosa, preferred_element_type=F32)
        weights = e[r]
        ds = (weights.astype(F32) * (dp - delta)).astype(BF)
        dq = dq + jnp.dot(kt[step + r], ds, preferred_element_type=F32)
        dkt[step + r] += lax.dot_general(qt, ds, nt, preferred_element_type=F32)
        dvt[step + r] += lax.dot_general(dos, weights, nt, preferred_element_type=F32)
    dqb = (dq * SCALE).astype(BF)
    dq_o[0] = dqb[:, :FR]
    dq_o[1] = dqb[:, FR:]

    @pl.when(step == 3)
    def _():
        for b in range(24):
            pair, half = b // 2, b % 2
            cols = slice(half * FR, (half + 1) * FR)
            dk_part = dkt[pair, :, cols] * SCALE
            dv_part = dvt[pair, :, cols]
            ref = (dlo_o, down_o, dhi_o)[b // 8]
            ref[b % 8, 0:HEAD, :] = dk_part.astype(ref.dtype)
            ref[b % 8, HEAD : 2 * HEAD, :] = dv_part.astype(ref.dtype)


def attention(bounds, own, lo, hi, do):
    pair = pl.BlockSpec((2, HEAD, FR), lambda i: (i, 0, 0))
    return pl.pallas_call(
        attn_kernel,
        grid=(4,),
        out_shape=(
            jax.ShapeDtypeStruct((SLAB, HEAD, FR), BF),
            jax.ShapeDtypeStruct((SLAB, HEAD, FR), BF),
            jax.ShapeDtypeStruct((SLAB, 2 * HEAD, FR), BF),
            jax.ShapeDtypeStruct((SLAB, 2 * HEAD, FR), F32),
            jax.ShapeDtypeStruct((SLAB, 2 * HEAD, FR), BF),
        ),
        in_specs=[SM, VM, VM, VM, VM],
        out_specs=(pair, pair, VM, VM, VM),
        scratch_shapes=[
            pltpu.VMEM((NB, HEAD, QB), BF),
            pltpu.VMEM((NB, HEAD, QB), BF),
            pltpu.VMEM((NB, QB, FR), BF),
            pltpu.VMEM((NB, QB, FR), BF),
            pltpu.VMEM((NKB, QB, QB), F32),
            pltpu.VMEM((NKB, QB, QB), BF),
            pltpu.VMEM((NB, HEAD, QB), F32),
            pltpu.VMEM((NB, HEAD, QB), F32),
        ],
        cost_estimate=pl.CostEstimate(
            flops=6 * 2 * 1024 * 2304 * 128, bytes_accessed=4_000_000, transcendentals=1024 * 2304
        ),
        name="attn",
    )(bounds, own, lo, hi, do)


CW = 256


def back_kernel(pos, prev, g, nxt, kern, gs_o, ext):
    ext[0:16, :] = prev[...].astype(F32)
    ext[16:144, :] = g[...].astype(F32)
    ext[144:160, :] = nxt[...].astype(F32)
    taps = kern[...].astype(F32)
    acc = jnp.zeros((FR, CW), F32)
    for t in range(TAPS):
        acc = acc + taps[t : t + 1, :] * ext[32 - t : 32 - t + FR, :]
    rows = pos[0] + lax.broadcasted_iota(jnp.int32, (FR, CW), 0)
    gs_o[...] = (ext[16:144, :] + jnp.where(rows < pos[1], acc, 0.0)).astype(BF)


def col(rows):
    return pl.BlockSpec((rows, CW), lambda i: (0, i))


def conv_back(pos, prev, g, nxt, kern):
    return pl.pallas_call(
        back_kernel,
        grid=(D // CW,),
        out_shape=jax.ShapeDtypeStruct((FR, D), BF),
        in_specs=[SM, col(16), col(FR), col(16), col(TAPS)],
        out_specs=col(FR),
        scratch_shapes=[pltpu.VMEM((160, CW), F32)],
        cost_estimate=pl.CostEstimate(flops=20_000_000, bytes_accessed=900_000, transcendentals=0),
        name="conv_back",
    )(pos, prev, g, nxt, kern)


def fore_kernel(pos, prev, mixed, nxt, g, kern, out_o, gk_o, ext):
    rows = pos[0] + lax.broadcasted_iota(jnp.int32, (FR, CW), 0)
    ext[0:16, :] = prev[...].astype(F32)
    ext[16:144, :] = jnp.where(rows < pos[1], mixed[...], 0.0).astype(BF).astype(F32)
    ext[144:160, :] = nxt[...].astype(F32)
    taps = kern[...].astype(F32)
    gf = g[...].astype(F32)
    acc = jnp.zeros((FR, CW), F32)
    for t in range(TAPS):
        moved = ext[t : t + FR, :]
        acc = acc + taps[t : t + 1, :] * moved
        gk_o[t : t + 1, :] = jnp.sum(gf * moved, axis=0, keepdims=True)
    out_o[...] = (mixed[...] + acc).astype(BF)


def conv_fore(pos, prev, mixed, nxt, g, kern):
    return pl.pallas_call(
        fore_kernel,
        grid=(D // CW,),
        out_shape=(jax.ShapeDtypeStruct((FR, D), BF), jax.ShapeDtypeStruct((TAPS, D), F32)),
        in_specs=[SM, col(16), col(FR), col(16), col(FR), col(TAPS)],
        out_specs=(col(FR), col(TAPS)),
        scratch_shapes=[pltpu.VMEM((160, CW), F32)],
        cost_estimate=pl.CostEstimate(flops=40_000_000, bytes_accessed=2_000_000, transcendentals=0),
        name="conv_fore",
    )(pos, prev, mixed, nxt, g, kern)


def gather_rows(part):
    zh, c = lax.axis_index("zh"), lax.axis_index("c")
    far = lax.ppermute(part, ("zh", "zl"), [(0, 3), (3, 0), (1, 2), (2, 1)])
    first = jnp.where(zh == 0, part, far)
    second = jnp.where(zh == 0, far, part)
    mine = jnp.stack([first, second])
    other = lax.ppermute(mine, "c", [(0, 1), (1, 0)])
    even = jnp.where(c == 0, mine, other)
    odd = jnp.where(c == 0, other, mine)
    return jnp.stack([even, odd], axis=1).reshape(4 * part.shape[0], part.shape[1])


def per_device(stream_in, queries, key_proj, values, w_out, conv_kernel, valid_length, grad_out):
    valid = valid_length[0]
    fs = lax.axis_index(("zh", "c"))
    slab = lax.axis_index(("zh", "c", "x"))
    device = lax.axis_index(AX)
    kernel_full = gather_rows(conv_kernel)
    g_prev = shift(grad_out[FR - 16 :], 1)
    g_next = shift(grad_out[:16], -1)
    weight_full = gather_rows(w_out)
    packed = lax.all_to_all(pack(queries, key_proj, values), SL, 0, 0, tiled=True)
    kv = packed[:, HEAD:, :]
    lo = shift(kv, 8)
    hi = shift(kv, -8)
    pos = jnp.stack([device * FR, valid]).astype(jnp.int32)
    grad_stream = conv_back(pos, g_prev, grad_out, g_next, kernel_full)
    grad_ctx_t = lax.dot_general(
        weight_full, grad_stream, (((1,), (1,)), ((), ())), preferred_element_type=F32
    ).astype(BF)
    do = lax.all_to_all(grad_ctx_t.reshape(HEADS, HEAD, FR), SL, 0, 0, tiled=True)
    start = (slab - 1) * 1024
    bounds = jnp.stack([jnp.maximum(0, -start), valid - start]).astype(jnp.int32)
    ctx, dq, dlo, down, dhi = attention(bounds, packed, lo, hi, do)
    from_hi = shift(dlo, -8)
    from_lo = shift(dhi, 8)
    both = lax.all_to_all(jnp.concatenate([ctx, dq], axis=1), SL, 0, 0, tiled=True)
    ctx_t = both[:, :HEAD, :].reshape(HEADS * HEAD, FR)
    grad_queries = both[:, HEAD:, :].reshape(HEADS * HEAD, FR).T
    mixed = stream_in.astype(F32) + lax.dot_general(
        ctx_t, weight_full, (((0,), (0,)), ((), ())), preferred_element_type=F32
    )
    live = (device * FR + jnp.arange(FR, dtype=jnp.int32) < valid)[:, None]
    masked = jnp.where(live, mixed, 0.0).astype(BF)
    m_prev = shift(masked[FR - 16 :], 1)
    m_next = shift(masked[:16], -1)
    grads = (down + from_hi.astype(F32) + from_lo.astype(F32)).astype(BF)
    grads = lax.all_to_all(grads, SL, 0, 0, tiled=True)
    grad_keys = grads[:, :HEAD, :].reshape(HEADS * HEAD, FR).T
    grad_values = grads[:, HEAD:, :].reshape(HEADS * HEAD, FR).T
    block_out, term_kernel = conv_fore(pos, m_prev, mixed, m_next, grad_out, kernel_full)
    term_weight = jnp.dot(ctx_t, grad_stream, preferred_element_type=F32)
    terms = jnp.concatenate(
        [
            term_weight.astype(BF).reshape(8, HEAD, D),
            term_kernel.astype(BF).reshape(8, 4, D),
            jnp.zeros((8, 4, D), BF),
        ],
        axis=1,
    )
    terms = lax.all_to_all(terms, SL, 0, 0, tiled=True)
    terms = jnp.sum(terms.astype(F32), axis=0).astype(BF)
    rows_w = terms[:HEAD].reshape(HEAD, 12, FR).transpose(1, 0, 2).reshape(16, 72, FR)
    rows_k = terms[HEAD : HEAD + 4].reshape(16, 3, FR)
    rows = jnp.concatenate([rows_w, rows_k, jnp.zeros((16, 5, FR), BF)], axis=1)
    pairs = []
    for f0 in range(4):
        for x in range(4):
            for p in range(8):
                pairs.append((f0 * 32 + x * 8 + p, (p // 2) * 32 + x * 8 + (p % 2) * 4 + f0))
    rows = lax.ppermute(rows, AX, pairs)
    rows = lax.all_to_all(rows, ("x", "y"), 0, 0, tiled=True)
    rows = jnp.sum(rows.astype(F32), axis=0).astype(BF)
    rows = jnp.broadcast_to(rows[None], (32, 80, FR))
    rows = lax.all_to_all(rows, SEQ, 0, 0, tiled=True).astype(F32)
    rows = rows.reshape(4, 2, 4, 80, FR).transpose(1, 0, 2, 3, 4).reshape(2, 16, 80, FR)
    grad_w_out = rows[:, :, :72].reshape(2, 12, HEAD, FR).transpose(0, 2, 1, 3).reshape(192, D)
    grad_kernel = rows[:, :, 72:75].reshape(8, D)
    return (block_out, grad_stream, grad_queries, grad_keys, grad_values, grad_w_out, grad_kernel)


def solution(mesh):
    fine = Mesh(mesh.devices.reshape(2, 2, 4, 2, 4), AX)
    split = P(AX, None)
    rows = P(("zh", "c"), None)
    return jax.shard_map(
        per_device,
        mesh=fine,
        in_specs=(split, split, split, split, rows, rows, P(), split),
        out_specs=(split, split, split, split, split, rows, rows),
        check_vma=False,
    )
```

time: 851 us -> 217 us (0.25)
  waiting for transfers between devices: 270 us -> 71.5 us
  blocking collectives: 174 us -> 0 us
  starting transfers between devices: 232 us -> 82.6 us
  local copies, waits for them, and re-layouts: 64.8 us -> 11.2 us
  matrix products: 43.3 us -> 4.63 us
  Pallas kernels: 0 us -> 33.4 us
  other arithmetic: 39 us -> 10.3 us
  between operations: 17.8 us -> 1.73 us
    ppermute x68 -> x13, starting transfers between devices: 232 us -> 31.6 us  [the longest x8 18.7 us: shift(): return lax.ppermute(value, AX, pairs)]
    psum x1 -> x0, blocking collectives: 157 us -> none  [per_device(): summed = lax.psum((term_weight, term_kernel), 'seq')]
    psum x1 -> x0, waiting for transfers between devices: 145 us -> none  [per_device(): summed = lax.psum((term_weight, term_kernel), 'seq')]
    ppermute x68 -> x13, waiting for transfers between devices: 95.1 us -> 8.42 us  [the longest x8 8.12 us: shift(): return lax.ppermute(value, AX, pairs)]
    all_to_all x0 -> x7, waiting for transfers between devices: none -> 63.1 us  [the longest x1 28.2 us: per_device(): terms = lax.all_to_all(terms, SL, 0, 0, tiled=True)]
    all_to_all x0 -> x7, starting transfers between devices: none -> 51.1 us  [the longest x1 24.8 us: per_device(): rows = lax.all_to_all(rows, ('x', 'y'), 0, 0, tiled=True)]
    dot_general x15 -> x3, matrix products: 43.3 us -> 4.63 us  [the longest x1 2.42 us: per_device(): lax.dot_general(ctx_t, weight_full, (((0,), (0,)), ((), ())), preferred_e...]
    pallas_call x0 -> x4, Pallas kernels: none -> 33.4 us  [the longest x1 16.5 us: attention(): pl.pallas_call(attn_kernel, grid=(4,), out_shape=(jax.ShapeDtypeStruct((S...]
  transfers between devices with their start and end apart: 72 -> 20, of which waited for: 23 -> 9; matrix products, arithmetic and copies ran while one was open for 13% -> 6% of each run, Pallas kernels for 0% -> 4%
where the time goes in v1:
time: 217 us; the launch traced here: 215 us
  starting transfers between devices  82.6 us (38%)
  waiting for transfers between devices  71.5 us (33%)
  Pallas kernels  33.4 us (15%)
  local copies, waits for them, and re-layouts  11.2 us (5%)
  other arithmetic  10.3 us (5%)
  matrix products  4.63 us (2%)
    all_to_all x1, waiting for transfers between devices, per_device(): terms = lax.all_to_all(terms, SL, 0, 0, tiled=True)  28.2 us
    all_to_all x1, starting transfers between devices, per_device(): rows = lax.all_to_all(rows, ('x', 'y'), 0, 0, tiled=True)  24.8 us
    ppermute x8, starting transfers between devices, shift(): return lax.ppermute(value, AX, pairs)  18.7 us
    pallas_call x1, Pallas kernels, attention(): pl.pallas_call(attn_kernel, grid=(4,), out_shape=(jax.ShapeDtypeStruct((S...  16.5 us
    all_to_all x1, waiting for transfers between devices, per_device(): lax.all_to_all(jnp.concatenate([ctx, dq], axis=1), SL, 0, 0, tiled=True)  9.43 us
    pallas_call x1, Pallas kernels, conv_fore(): pl.pallas_call(fore_kernel, grid=(D // CW,), out_shape=(jax.ShapeDtypeStr...  9.13 us
    ppermute x2, starting transfers between devices, gather_rows(): far = lax.ppermute(part, ('zh', 'zl'), [(0, 3), (3, 0), (1, 2), (2, 1)])  8.51 us
    all_to_all x1, waiting for transfers between devices, per_device(): rows = lax.all_to_all(rows, SEQ, 0, 0, tiled=True).astype(F32)  8.24 us
  transfers between devices with their start and end apart: 20, of which 9 were waited for; matrix products, arithmetic and copies ran while one was open for 6% of the time, Pallas kernels for 4%

profile of v1, /device:TPU:0, one launch (start us, length us, event | category | flops | bytes accessed | tf_op | source)
XLA Modules:
  0.0 215.4 jit_solution(6303733772123203539)
XLA Ops:
  0.7 4.2 %collective-permute-start.2 = (bf16[192,1536]{1,0:T(8,128)(2,1)}, bf16[192,1536]{1,0:T(8,128)(2,1)S(1)}, u32[]{:S(2)}, u32[]{:S(2)}) collective-permute-start(bf16[192,1536]{1,0:T(8,128)(2,1)} %param.12), channel_id=1, source_target_pairs={{0,68},{68,0},{4,64},{64,4},{1,69},{69,1},{5,65},{65,5},{2,70},{70... | collective-permute-start | bytes 1769480 | tf_op jit(solution)/shard_map/ppermute | solution.py:232
  4.9 2.2 pack.1
  7.0 4.5 %all-to-all-start = ((bf16[8,288,128]{2,1,0:T(8,128)(2,1)}), bf16[8,288,128]{2,1,0:T(8,128)(2,1)S(1)}, u32[]{:S(2)}, u32[]{:S(2)}) async-start(bf16[8,288,128]{2,1,0:T(8,128)(2,1)} %pack.1), calls=%async_computation | async-start | bytes 1179648 | tf_op jit(solution)/shard_map/all_to_all | solution.py:251
  11.5 0.8 fusion.3
  12.3 3.9 %collective-permute-start.4 = (bf16[16,1536]{1,0:T(8,128)(2,1)S(1)}, bf16[16,1536]{1,0:T(8,128)(2,1)S(1)}, u32[]{:S(2)}, u32[]{:S(2)}) collective-permute-start(bf16[16,1536]{1,0:T(8,128)(2,1)S(1)} %get-tuple-element.32), channel_id=1, source_target_pairs={{0,1},{1,2},{2,3},{3,4},{4,5},{5,6},{6,7},{7,8},{8,9},{9,10},{10,1... | collective-permute-start | bytes 147464 | tf_op jit(solution)/shard_map/ppermute | solution.py:33
  16.3 1.3 collective-permute-start.5
  17.6 4.3 %collective-permute-start.6 = (bf16[8,1536]{1,0:T(8,128)(2,1)S(1)}, bf16[8,1536]{1,0:T(8,128)(2,1)S(1)}, u32[]{:S(2)}, u32[]{:S(2)}) collective-permute-start(bf16[8,1536]{1,0:T(8,128)(2,1)S(1)} %copy-done.9), channel_id=1, source_target_pairs={{0,68},{68,0},{4,64},{64,4},{1,69},{69,1},{5,65},{65,5},{2,70},{70... | collective-permute-start | bytes 73736 | tf_op jit(solution)/shard_map/ppermute | solution.py:232
  22.5 0.1 select_bitcast_fusion.3
  22.6 1.1 pad_maximum_fusion.1
  23.7 0.9 collective-permute-start.3
  24.6 2.1 collective-permute-start.7
  26.7 0.6 pad_add_fusion.pos
  27.3 0.3 collective-permute-done.7
  27.6 0.7 copy.28
  28.3 0.6 copy-done.5
  28.9 5.7 %conv_back.1 = bf16[128,1536]{1,0:T(8,128)(2,1)} custom-call(s32[2]{0:T(128)} %pad_add_fusion.pos, bf16[16,1536]{1,0:T(8,128)(2,1)} %copy-done.5, bf16[128,1536]{1,0:T(8,128)(2,1)} %g.3, bf16[16,1536]{1,0:T(8,128)(2,1)} %copy-done.6, bf16[32,1536]{1,0:T(8,128)(2,1)} %bitcast.68), custom_call_target="tpu_custom_call" | custom-call | flops 20000000 | bytes 900000 | tf_op jit(solution)/shard_map/conv_back/pallas_call | solution.py:190
  34.6 4.2 %collective-permute-start = (bf16[8,192,128]{2,1,0:T(8,128)(2,1)S(1)}, bf16[8,192,128]{2,1,0:T(8,128)(2,1)}, u32[]{:S(2)}, u32[]{:S(2)}) collective-permute-start(bf16[8,192,128]{2,1,0:T(8,128)(2,1)S(1)} %slice.52), channel_id=1, source_target_pairs={{0,8},{1,9},{2,10},{3,11},{4,12},{5,13},{6,14},{7,15},{8,16},{9,17... | collective-permute-start | bytes 1179656 | tf_op jit(solution)/shard_map/ppermute | solution.py:33
  38.9 1.3 collective-permute-start.1
  40.2 0.2 select_bitcast_fusion.1
  40.4 0.2 pad_maximum_fusion
  40.6 0.8 copy-done.1
  41.4 1.5 convolution_convert_fusion.1
  42.8 3.4 %all-to-all-start.1 = ((bf16[8,96,128]{2,1,0:T(8,128)(2,1)}), bf16[8,96,128]{2,1,0:T(8,128)(2,1)S(1)}, u32[]{:S(2)}, u32[]{:S(2)}) async-start(bf16[8,96,128]{2,1,0:T(8,128)(2,1)} %bitcast.15), calls=%async_computation.1 | async-start | bytes 393216 | tf_op jit(solution)/shard_map/all_to_all | solution.py:260
  46.2 0.6 pad_add_fusion.1.bounds
  46.8 4.2 %collective-permute-done.1.hi = bf16[8,192,128]{2,1,0:T(8,128)(2,1)} collective-permute-done((bf16[8,192,128]{2,1,0:T(8,128)(2,1)S(1)}, bf16[8,192,128]{2,1,0:T(8,128)(2,1)}, u32[]{:S(2)}, u32[]{:S(2)}) %collective-permute-start.1) | collective-permute-done | bytes 393248 | tf_op jit(solution)/shard_map/ppermute | solution.py:33
  51.0 2.4 %all-to-all-done.1.do = bf16[8,96,128]{2,1,0:T(8,128)(2,1)S(1)} async-done(((bf16[8,96,128]{2,1,0:T(8,128)(2,1)}), bf16[8,96,128]{2,1,0:T(8,128)(2,1)S(1)}, u32[]{:S(2)}, u32[]{:S(2)}) %all-to-all-start.1) | async-done | bytes 196640 | tf_op jit(solution)/shard_map/all_to_all | solution.py:260
  53.5 0.7 copy-done.4
  54.2 16.5 %attn.1 = (bf16[8,96,128]{2,1,0:T(8,128)(2,1)}, bf16[8,96,128]{2,1,0:T(8,128)(2,1)}, bf16[8,192,128]{2,1,0:T(8,128)(2,1)}, f32[8,192,128]{2,1,0:T(8,128)}, bf16[8,192,128]{2,1,0:T(8,128)(2,1)}) custom-call(s32[2]{0:T(128)} %pad_add_fusion.1.bounds, bf16[8,288,128]{2,1,0:T(8,128)(2,1)} %copy-done, bf16[8,192,128]{2,1,0:T(8,128)(2,1)} %collective-permute-done.lo, ...), custom_call_target="tpu_custom_call" | custom-call | flops 3623878656 | bytes 4000000 | tf_op jit(solution)/shard_map/attn/pallas_call | solution.py:141
  70.6 1.8 pad_maximum_fusion.2
  72.4 3.5 %all-to-all-start.2 = ((bf16[8,192,128]{2,1,0:T(8,128)(2,1)}), bf16[8,192,128]{2,1,0:T(8,128)(2,1)S(1)}, u32[]{:S(2)}, u32[]{:S(2)}) async-start(bf16[8,192,128]{2,1,0:T(8,128)(2,1)} %pad_maximum_fusion.2), calls=%async_computation.2 | async-start | bytes 786432 | tf_op jit(solution)/shard_map/all_to_all | solution.py:266
  76.0 9.4 %all-to-all-done.2 = bf16[8,192,128]{2,1,0:T(8,128)(2,1)S(1)} async-done(((bf16[8,192,128]{2,1,0:T(8,128)(2,1)}), bf16[8,192,128]{2,1,0:T(8,128)(2,1)S(1)}, u32[]{:S(2)}, u32[]{:S(2)}) %all-to-all-start.2) | async-done | bytes 393248 | tf_op jit(solution)/shard_map/all_to_all | solution.py:266
  85.5 2.4 %select_convert_fusion = (bf16[128,1536]{1,0:T(8,128)(2,1)S(1)}, f32[128,1536]{1,0:T(8,128)}) fusion(pred[128]{0:T(512)(128)(4,1)S(1)} %add_compare_fusion, bf16[768,128]{1,0:T(8,128)(2,1)S(1)} %bitcast.63, bf16[768,1536]{1,0:T(8,128)(2,1)S(1)} %bitcast.56, bf16[128,1536]{1,0:T(8,128)(2,1)} %param.8), kind=kOutput, calls=%fused_computation.11 | convolution fusion | flops 302579712 | bytes 4128896 | tf_op jit(solution)/shard_map/dot_general | solution.py:269
  87.9 2.8 %collective-permute-start.8 = (bf16[16,1536]{1,0:T(8,128)(2,1)S(1)}, bf16[16,1536]{1,0:T(8,128)(2,1)S(1)}, u32[]{:S(2)}, u32[]{:S(2)}) collective-permute-start(bf16[16,1536]{1,0:T(8,128)(2,1)S(1)} %get-tuple-element.30), channel_id=1, source_target_pairs={{0,1},{1,2},{2,3},{3,4},{4,5},{5,6},{6,7},{7,8},{8,9},{9,10},{10,1... | collective-permute-start | bytes 147464 | tf_op jit(solution)/shard_map/ppermute | solution.py:33
  90.7 1.3 collective-permute-start.9
  92.0 0.8 convolution_convert_fusion
  92.7 3.9 %collective-permute-done.9.nxt = bf16[16,1536]{1,0:T(8,128)(2,1)S(1)} collective-permute-done((bf16[16,1536]{1,0:T(8,128)(2,1)S(1)}, bf16[16,1536]{1,0:T(8,128)(2,1)S(1)}, u32[]{:S(2)}, u32[]{:S(2)}) %collective-permute-start.9) | collective-permute-done | bytes 49184 | tf_op jit(solution)/shard_map/ppermute | solution.py:33
  96.6 0.6 copy-done.8
  97.3 9.1 %conv_fore.1 = (bf16[128,1536]{1,0:T(8,128)(2,1)}, f32[32,1536]{1,0:T(8,128)}) custom-call(s32[2]{0:T(128)} %pad_add_fusion.pos, bf16[16,1536]{1,0:T(8,128)(2,1)} %copy-done.7, f32[128,1536]{1,0:T(8,128)} %get-tuple-element.38.mixed, bf16[16,1536]{1,0:T(8,128)(2,1)} %copy-done.8, bf16[128,1536]{1,0:T(8,128)(2,1)} %g.3, bf16[32,1536]{1,0:T(8,128)(2,1)} %bitcast.69), custom_call_target="tpu_custom_call" | custom-call | flops 40000000 | bytes 2000000 | tf_op jit(solution)/shard_map/conv_fore/pallas_call | solution.py:218
  106.4 0.9 convert_element_type.36
  107.4 2.1 maximum_maximum_fusion
  109.4 7.6 %all-to-all-start.4 = ((bf16[8,104,1536]{2,1,0:T(8,128)(2,1)}), bf16[8,104,1536]{2,1,0:T(8,128)(2,1)S(1)}, u32[]{:S(2)}, u32[]{:S(2)}) async-start(bf16[8,104,1536]{2,1,0:T(8,128)(2,1)} %maximum_maximum_fusion), calls=%async_computation.4 | async-start | bytes 5111808 | tf_op jit(solution)/shard_map/all_to_all | solution.py:290
  117.2 2.7 %collective-permute-start.11 = (bf16[8,192,128]{2,1,0:T(8,128)(2,1)}, bf16[8,192,128]{2,1,0:T(8,128)(2,1)S(1)}, u32[]{:S(2)}, u32[]{:S(2)}) collective-permute-start(bf16[8,192,128]{2,1,0:T(8,128)(2,1)} %get-tuple-element.19), channel_id=1, source_target_pairs={{0,8},{1,9},{2,10},{3,11},{4,12},{5,13},{6,14},{7,15},{8,16},{9,17... | collective-permute-start | bytes 1179656 | tf_op jit(solution)/shard_map/ppermute | solution.py:33
  119.8 1.3 collective-permute-start.10
  121.1 28.2 %all-to-all-done.4 = bf16[8,104,1536]{2,1,0:T(8,128)(2,1)S(1)} async-done(((bf16[8,104,1536]{2,1,0:T(8,128)(2,1)}), bf16[8,104,1536]{2,1,0:T(8,128)(2,1)S(1)}, u32[]{:S(2)}, u32[]{:S(2)}) %all-to-all-start.4) | async-done | bytes 2555936 | tf_op jit(solution)/shard_map/all_to_all | solution.py:290
  149.3 0.5 reduce_sum.24
  149.8 0.2 reshape.84
  150.2 0.1 maximum_maximum_fusion.1
  150.3 1.4 collective-permute-start.12
  151.7 24.8 %all-to-all-start.5 = ((bf16[16,80,128]{2,1,0:T(8,128)(2,1)}), bf16[16,80,128]{2,1,0:T(8,128)(2,1)S(1)}, u32[]{:S(2)}, u32[]{:S(2)}) async-start(bf16[16,80,128]{2,1,0:T(8,128)(2,1)} %collective-permute-done.12), calls=%async_computation.5 | async-start | bytes 655360 | tf_op jit(solution)/shard_map/all_to_all | solution.py:301
  176.5 1.9 add_convert_fusion
  178.4 6.9 %all-to-all-done.5 = bf16[16,80,128]{2,1,0:T(8,128)(2,1)S(1)} async-done(((bf16[16,80,128]{2,1,0:T(8,128)(2,1)}), bf16[16,80,128]{2,1,0:T(8,128)(2,1)S(1)}, u32[]{:S(2)}, u32[]{:S(2)}) %all-to-all-start.5) | async-done | bytes 327712 | tf_op jit(solution)/shard_map/all_to_all | solution.py:301
  185.3 3.5 %all-to-all-start.3 = ((bf16[8,192,128]{2,1,0:T(8,128)(2,1)}), bf16[8,192,128]{2,1,0:T(8,128)(2,1)S(1)}, u32[]{:S(2)}, u32[]{:S(2)}) async-start(bf16[8,192,128]{2,1,0:T(8,128)(2,1)} %add_convert_fusion), calls=%async_computation.3 | async-start | bytes 786432 | tf_op jit(solution)/shard_map/all_to_all | solution.py:277
  188.8 7.9 %all-to-all-done.3 = bf16[8,192,128]{2,1,0:T(8,128)(2,1)S(1)} async-done(((bf16[8,192,128]{2,1,0:T(8,128)(2,1)}), bf16[8,192,128]{2,1,0:T(8,128)(2,1)S(1)}, u32[]{:S(2)}, u32[]{:S(2)}) %all-to-all-start.3) | async-done | bytes 393248 | tf_op jit(solution)/shard_map/all_to_all | solution.py:277
  196.7 0.9 broadcast_in_dim.29
  197.6 3.9 %all-to-all-start.6 = ((bf16[32,80,128]{2,1,0:T(8,128)(2,1)}), bf16[32,80,128]{2,1,0:T(8,128)(2,1)S(1)}, u32[]{:S(2)}, u32[]{:S(2)}) async-start(bf16[32,80,128]{2,1,0:T(8,128)(2,1)} %broadcast_in_dim.29), calls=%async_computation.6 | async-start | bytes 1310720 | tf_op jit(solution)/shard_map/all_to_all | solution.py:304
  201.5 0.8 copy.29
  202.4 0.8 copy.30
  203.2 0.8 copy.31
  204.0 8.2 %all-to-all-done.6 = bf16[32,80,128]{2,1,0:T(8,128)(2,1)S(1)} async-done(((bf16[32,80,128]{2,1,0:T(8,128)(2,1)}), bf16[32,80,128]{2,1,0:T(8,128)(2,1)S(1)}, u32[]{:S(2)}, u32[]{:S(2)}) %all-to-all-start.6) | async-done | bytes 655392 | tf_op jit(solution)/shard_map/all_to_all | solution.py:304
  212.2 0.1 convert_bitcast_fusion
  212.4 0.1 copy.33
  212.6 0.7 copy.34
  213.3 1.5 copy.37
  214.7 0.6 reshape.92
  (48 shorter events, 0.7 us)
Async XLA Ops:
  0.6 21.9 %copy-start.3 = (bf16[192,1536]{1,0:T(8,128)(2,1)S(1)}, bf16[192,1536]{1,0:T(8,128)(2,1)}, u32[]{:S(2)}) copy-start(bf16[192,1536]{1,0:T(8,128)(2,1)} %param.12) | copy-start | bytes 1769476
  0.6 16.9 %copy-start.9 = (bf16[8,1536]{1,0:T(8,128)(2,1)S(1)}, bf16[8,1536]{1,0:T(8,128)(2,1)}, u32[]{:S(2)}) copy-start(bf16[8,1536]{1,0:T(8,128)(2,1)} %param.13) | copy-start | bytes 73732
  0.7 21.9 %collective-permute-start.2 = (bf16[192,1536]{1,0:T(8,128)(2,1)}, bf16[192,1536]{1,0:T(8,128)(2,1)S(1)}, u32[]{:S(2)}, u32[]{:S(2)}) collective-permute-start(bf16[192,1536]{1,0:T(8,128)(2,1)} %param.12), channel_id=1, source_target_pairs={{0,68},{68,0},{4,64},{64,4},{1,69},{69,1},{5,65},{65,5},{2,70},{70... | collective-permute-start | bytes 1769480 | tf_op jit(solution)/shard_map/ppermute | solution.py:232
  7.0 27.6 %all-to-all-start = ((bf16[8,288,128]{2,1,0:T(8,128)(2,1)}), bf16[8,288,128]{2,1,0:T(8,128)(2,1)S(1)}, u32[]{:S(2)}, u32[]{:S(2)}) async-start(bf16[8,288,128]{2,1,0:T(8,128)(2,1)} %pack.1), calls=%async_computation | async-start | bytes 1179648 | tf_op jit(solution)/shard_map/all_to_all | solution.py:251
  12.3 15.9 %collective-permute-start.4 = (bf16[16,1536]{1,0:T(8,128)(2,1)S(1)}, bf16[16,1536]{1,0:T(8,128)(2,1)S(1)}, u32[]{:S(2)}, u32[]{:S(2)}) collective-permute-start(bf16[16,1536]{1,0:T(8,128)(2,1)S(1)} %get-tuple-element.32), channel_id=1, source_target_pairs={{0,1},{1,2},{2,3},{3,4},{4,5},{5,6},{6,7},{7,8},{8,9},{9,10},{10,1... | collective-permute-start | bytes 147464 | tf_op jit(solution)/shard_map/ppermute | solution.py:33
  16.3 12.0 %collective-permute-start.5 = (bf16[16,1536]{1,0:T(8,128)(2,1)S(1)}, bf16[16,1536]{1,0:T(8,128)(2,1)S(1)}, u32[]{:S(2)}, u32[]{:S(2)}) collective-permute-start(bf16[16,1536]{1,0:T(8,128)(2,1)S(1)} %get-tuple-element.31), channel_id=1, source_target_pairs={{1,0},{2,1},{3,2},{4,3},{5,4},{6,5},{7,6},{8,7},{9,8},{10,9},{11,1... | collective-permute-start | bytes 147464 | tf_op jit(solution)/shard_map/ppermute | solution.py:33
  17.6 7.0 %collective-permute-start.6 = (bf16[8,1536]{1,0:T(8,128)(2,1)S(1)}, bf16[8,1536]{1,0:T(8,128)(2,1)S(1)}, u32[]{:S(2)}, u32[]{:S(2)}) collective-permute-start(bf16[8,1536]{1,0:T(8,128)(2,1)S(1)} %copy-done.9), channel_id=1, source_target_pairs={{0,68},{68,0},{4,64},{64,4},{1,69},{69,1},{5,65},{65,5},{2,70},{70... | collective-permute-start | bytes 73736 | tf_op jit(solution)/shard_map/ppermute | solution.py:232
  23.7 16.4 %collective-permute-start.3 = (bf16[2,192,1536]{2,1,0:T(8,128)(2,1)}, bf16[2,192,1536]{2,1,0:T(8,128)(2,1)S(1)}, u32[]{:S(2)}, u32[]{:S(2)}) collective-permute-start(bf16[2,192,1536]{2,1,0:T(8,128)(2,1)} %pad_maximum_fusion.1), channel_id=1, source_target_pairs={{0,32},{32,0},{1,33},{33,1},{2,34},{34,2},{3,35},{35,3},{4,36},{36... | collective-permute-start | bytes 3538952 | tf_op jit(solution)/shard_map/ppermute | solution.py:236
  24.6 2.9 %collective-permute-start.7 = (bf16[2,8,1536]{2,1,0:T(8,128)(2,1)S(1)}, bf16[2,8,1536]{2,1,0:T(8,128)(2,1)S(1)}, u32[]{:S(2)}, u32[]{:S(2)}) collective-permute-start(bf16[2,8,1536]{2,1,0:T(8,128)(2,1)S(1)} %pad_maximum_fusion.4), channel_id=1, source_target_pairs={{0,32},{32,0},{1,33},{33,1},{2,34},{34,2},{3,35},{35,3},{4,36},{36... | collective-permute-start | bytes 147464 | tf_op jit(solution)/shard_map/ppermute | solution.py:236
  28.3 0.6 copy-start.5
  28.3 0.6 copy-start.6
  34.6 5.7 %copy-start = (bf16[8,288,128]{2,1,0:T(8,128)(2,1)}, bf16[8,288,128]{2,1,0:T(8,128)(2,1)S(1)}, u32[]{:S(2)}) copy-start(bf16[8,288,128]{2,1,0:T(8,128)(2,1)S(1)} %all-to-all-done.own) | copy-start | bytes 1769476
  34.6 12.2 %collective-permute-start = (bf16[8,192,128]{2,1,0:T(8,128)(2,1)S(1)}, bf16[8,192,128]{2,1,0:T(8,128)(2,1)}, u32[]{:S(2)}, u32[]{:S(2)}) collective-permute-start(bf16[8,192,128]{2,1,0:T(8,128)(2,1)S(1)} %slice.52), channel_id=1, source_target_pairs={{0,8},{1,9},{2,10},{3,11},{4,12},{5,13},{6,14},{7,15},{8,16},{9,17... | collective-permute-start | bytes 1179656 | tf_op jit(solution)/shard_map/ppermute | solution.py:33
  38.9 12.1 %collective-permute-start.1 = (bf16[8,192,128]{2,1,0:T(8,128)(2,1)S(1)}, bf16[8,192,128]{2,1,0:T(8,128)(2,1)}, u32[]{:S(2)}, u32[]{:S(2)}) collective-permute-start(bf16[8,192,128]{2,1,0:T(8,128)(2,1)S(1)} %slice.52), channel_id=1, source_target_pairs={{8,0},{9,1},{10,2},{11,3},{12,4},{13,5},{14,6},{15,7},{16,8},{17,9... | collective-permute-start | bytes 1179656 | tf_op jit(solution)/shard_map/ppermute | solution.py:33
  40.4 1.0 copy-start.1
  42.8 10.7 %all-to-all-start.1 = ((bf16[8,96,128]{2,1,0:T(8,128)(2,1)}), bf16[8,96,128]{2,1,0:T(8,128)(2,1)S(1)}, u32[]{:S(2)}, u32[]{:S(2)}) async-start(bf16[8,96,128]{2,1,0:T(8,128)(2,1)} %bitcast.15), calls=%async_computation.1 | async-start | bytes 393216 | tf_op jit(solution)/shard_map/all_to_all | solution.py:260
  53.5 0.7 copy-start.4
  72.4 13.0 %all-to-all-start.2 = ((bf16[8,192,128]{2,1,0:T(8,128)(2,1)}), bf16[8,192,128]{2,1,0:T(8,128)(2,1)S(1)}, u32[]{:S(2)}, u32[]{:S(2)}) async-start(bf16[8,192,128]{2,1,0:T(8,128)(2,1)} %pad_maximum_fusion.2), calls=%async_computation.2 | async-start | bytes 786432 | tf_op jit(solution)/shard_map/all_to_all | solution.py:266
  87.9 4.8 %collective-permute-start.8 = (bf16[16,1536]{1,0:T(8,128)(2,1)S(1)}, bf16[16,1536]{1,0:T(8,128)(2,1)S(1)}, u32[]{:S(2)}, u32[]{:S(2)}) collective-permute-start(bf16[16,1536]{1,0:T(8,128)(2,1)S(1)} %get-tuple-element.30), channel_id=1, source_target_pairs={{0,1},{1,2},{2,3},{3,4},{4,5},{5,6},{6,7},{7,8},{8,9},{9,10},{10,1... | collective-permute-start | bytes 147464 | tf_op jit(solution)/shard_map/ppermute | solution.py:33
  90.7 6.0 %collective-permute-start.9 = (bf16[16,1536]{1,0:T(8,128)(2,1)S(1)}, bf16[16,1536]{1,0:T(8,128)(2,1)S(1)}, u32[]{:S(2)}, u32[]{:S(2)}) collective-permute-start(bf16[16,1536]{1,0:T(8,128)(2,1)S(1)} %get-tuple-element.29), channel_id=1, source_target_pairs={{1,0},{2,1},{3,2},{4,3},{5,4},{6,5},{7,6},{8,7},{9,8},{10,9},{11,1... | collective-permute-start | bytes 147464 | tf_op jit(solution)/shard_map/ppermute | solution.py:33
  92.7 3.9 %copy-start.7 = (bf16[16,1536]{1,0:T(8,128)(2,1)}, bf16[16,1536]{1,0:T(8,128)(2,1)S(1)}, u32[]{:S(2)}) copy-start(bf16[16,1536]{1,0:T(8,128)(2,1)S(1)} %collective-permute-done.8.prev) | copy-start | bytes 147460
  96.6 0.6 copy-start.8
  109.4 39.9 %all-to-all-start.4 = ((bf16[8,104,1536]{2,1,0:T(8,128)(2,1)}), bf16[8,104,1536]{2,1,0:T(8,128)(2,1)S(1)}, u32[]{:S(2)}, u32[]{:S(2)}) async-start(bf16[8,104,1536]{2,1,0:T(8,128)(2,1)} %maximum_maximum_fusion), calls=%async_computation.4 | async-start | bytes 5111808 | tf_op jit(solution)/shard_map/all_to_all | solution.py:290
  117.2 59.3 %collective-permute-start.11 = (bf16[8,192,128]{2,1,0:T(8,128)(2,1)}, bf16[8,192,128]{2,1,0:T(8,128)(2,1)S(1)}, u32[]{:S(2)}, u32[]{:S(2)}) collective-permute-start(bf16[8,192,128]{2,1,0:T(8,128)(2,1)} %get-tuple-element.19), channel_id=1, source_target_pairs={{0,8},{1,9},{2,10},{3,11},{4,12},{5,13},{6,14},{7,15},{8,16},{9,17... | collective-permute-start | bytes 1179656 | tf_op jit(solution)/shard_map/ppermute | solution.py:33
  119.8 56.6 %collective-permute-start.10 = (bf16[8,192,128]{2,1,0:T(8,128)(2,1)}, bf16[8,192,128]{2,1,0:T(8,128)(2,1)}, u32[]{:S(2)}, u32[]{:S(2)}) collective-permute-start(bf16[8,192,128]{2,1,0:T(8,128)(2,1)} %get-tuple-element.18), channel_id=1, source_target_pairs={{8,0},{9,1},{10,2},{11,3},{12,4},{13,5},{14,6},{15,7},{16,8},{17,9... | collective-permute-start | bytes 1179656 | tf_op jit(solution)/shard_map/ppermute | solution.py:33
  149.8 26.7 %copy-start.2 = (f32[8,192,128]{2,1,0:T(8,128)S(1)}, f32[8,192,128]{2,1,0:T(8,128)}, u32[]{:S(2)}) copy-start(f32[8,192,128]{2,1,0:T(8,128)} %get-tuple-element.17) | copy-start | bytes 2359300
  150.3 1.4 collective-permute-start.12
  151.7 33.6 %all-to-all-start.5 = ((bf16[16,80,128]{2,1,0:T(8,128)(2,1)}), bf16[16,80,128]{2,1,0:T(8,128)(2,1)S(1)}, u32[]{:S(2)}, u32[]{:S(2)}) async-start(bf16[16,80,128]{2,1,0:T(8,128)(2,1)} %collective-permute-done.12), calls=%async_computation.5 | async-start | bytes 655360 | tf_op jit(solution)/shard_map/all_to_all | solution.py:301
  185.3 11.4 %all-to-all-start.3 = ((bf16[8,192,128]{2,1,0:T(8,128)(2,1)}), bf16[8,192,128]{2,1,0:T(8,128)(2,1)S(1)}, u32[]{:S(2)}, u32[]{:S(2)}) async-start(bf16[8,192,128]{2,1,0:T(8,128)(2,1)} %add_convert_fusion), calls=%async_computation.3 | async-start | bytes 786432 | tf_op jit(solution)/shard_map/all_to_all | solution.py:277
  197.6 14.7 %all-to-all-start.6 = ((bf16[32,80,128]{2,1,0:T(8,128)(2,1)}), bf16[32,80,128]{2,1,0:T(8,128)(2,1)S(1)}, u32[]{:S(2)}, u32[]{:S(2)}) async-start(bf16[32,80,128]{2,1,0:T(8,128)(2,1)} %broadcast_in_dim.29), calls=%async_computation.6 | async-start | bytes 1310720 | tf_op jit(solution)/shard_map/all_to_all | solution.py:304

commit v2 on v1

v2 whole, which is shorter than its diff:
```python
import jax
import jax.numpy as jnp
from jax import lax
from jax.experimental import pallas as pl
from jax.experimental.pallas import tpu as pltpu
from jax.sharding import Mesh, PartitionSpec as P

HEADS = 8
HEAD = 96
TAPS = 32
WIN = 1024
D = 1536
FR = 128
SLAB = 8
QB = 256
NKB = 9
NB = 12
NEG = -1e30
LOG2E = 1.4426950408889634
SCALE = HEAD ** -0.5
AX = ("zh", "c", "x", "zl", "y")
SEQ = ("x", "zl", "y")
SL = ("zl", "y")
BF = jnp.bfloat16
F32 = jnp.float32
VM = pl.BlockSpec(memory_space=pltpu.VMEM)
SM = pl.BlockSpec(memory_space=pltpu.SMEM)


def shift(value, steps):
    n = 128
    pairs = [(i, i + steps) for i in range(max(0, -steps), min(n, n - steps))]
    return lax.ppermute(value, AX, pairs)


ORDER = tuple(2 * (p % 4) + p // 4 for p in range(SLAB))


def pack_kernel(q, k, v, out):
    for n, ref in enumerate((q, k, v)):
        turned = ref[...].T
        for p, h in enumerate(ORDER):
            out[p, n * HEAD : (n + 1) * HEAD, :] = turned[h * HEAD : (h + 1) * HEAD, :]


def pack(q, k, v):
    return pl.pallas_call(
        pack_kernel,
        out_shape=jax.ShapeDtypeStruct((HEADS, 3 * HEAD, FR), BF),
        in_specs=[VM] * 3,
        out_specs=VM,
        cost_estimate=pl.CostEstimate(flops=0, bytes_accessed=1_200_000, transcendentals=0),
        name="pack",
    )(q, k, v)


def unpack_kernel(got, q_o, k_o, v_o):
    for n, ref in enumerate((q_o, k_o, v_o)):
        parts = [got[ORDER.index(h), n * HEAD : (n + 1) * HEAD, :] for h in range(HEADS)]
        ref[...] = jnp.concatenate(parts, axis=0).T


def unpack(got):
    return pl.pallas_call(
        unpack_kernel,
        out_shape=(jax.ShapeDtypeStruct((FR, HEADS * HEAD), BF),) * 3,
        in_specs=[VM],
        out_specs=(VM,) * 3,
        cost_estimate=pl.CostEstimate(flops=0, bytes_accessed=1_200_000, transcendentals=0),
        name="unpack",
    )(got)


def window_block(b, own, lo, hi):
    if b < 8:
        return lo[b, 0:HEAD, :], lo[b, HEAD : 2 * HEAD, :]
    if b < 16:
        return own[b - 8, HEAD : 2 * HEAD, :], own[b - 8, 2 * HEAD : 3 * HEAD, :]
    return hi[b - 16, 0:HEAD, :], hi[b - 16, HEAD : 2 * HEAD, :]


def fore_attn_kernel(bounds, own, lo, hi, ctx_o, e_o, inv_o, vt, ka, s):
    step = pl.program_id(0)

    @pl.when(step == 0)
    def _():
        first, last = bounds[0], bounds[1]
        pad_rows = lax.broadcasted_iota(jnp.int32, (32, FR), 0)
        lanes = lax.broadcasted_iota(jnp.int32, (32, FR), 1)
        for b in range(24):
            kb, vb = window_block(b, own, lo, hi)
            pair, half = b // 2, b % 2
            cols = slice(half * FR, (half + 1) * FR)
            vt[pair, :, cols] = vb
            place = lanes + b * FR
            hidden = (pad_rows == 0) & ((place < first) | (place >= last))
            extra = jnp.where(hidden, NEG, 0.0).astype(BF)
            ka[pair, cols, :] = jnp.concatenate([kb, extra], axis=0).T

    qt = jnp.concatenate([own[2 * step, 0:HEAD, :], own[2 * step + 1, 0:HEAD, :]], axis=1)
    ones = jnp.where(lax.broadcasted_iota(jnp.int32, (32, QB), 0) == 0, 1.0, 0.0).astype(BF)
    qa = jnp.concatenate([qt, ones], axis=0)
    kk = lax.broadcasted_iota(jnp.int32, (QB, QB), 0)
    qq = lax.broadcasted_iota(jnp.int32, (QB, QB), 1)
    top = None
    for r in range(NKB):
        part = jnp.dot(ka[step + r], qa, preferred_element_type=F32)
        if r == 0:
            part = jnp.where(kk >= qq, part, NEG)
        if r == NKB - 1:
            part = jnp.where(kk <= qq, part, NEG)
        s[r] = part
        peak = jnp.max(part, axis=0, keepdims=True)
        top = peak if top is None else jnp.maximum(top, peak)
    shift_top = top * (SCALE * LOG2E)
    total = jnp.zeros((1, QB), F32)
    out_t = jnp.zeros((HEAD, QB), F32)
    for r in range(NKB):
        part = jnp.exp2(s[r] * (SCALE * LOG2E) - shift_top)
        total = total + jnp.sum(part, axis=0, keepdims=True)
        rounded = part.astype(BF)
        e_o[0, r] = rounded
        out_t = out_t + jnp.dot(vt[step + r], rounded, preferred_element_type=F32)
    inverse = 1.0 / total
    ctx = (out_t * inverse).astype(BF)
    ctx_o[0] = ctx[:, :FR]
    ctx_o[1] = ctx[:, FR:]
    inv_o[0] = inverse


PAIR = pl.BlockSpec((2, HEAD, FR), lambda i: (i, 0, 0))
E_SPEC = pl.BlockSpec((1, NKB, QB, QB), lambda i: (i, 0, 0, 0))
I_SPEC = pl.BlockSpec((1, 1, QB), lambda i: (i, 0, 0))


def attn_fore(bounds, own, lo, hi):
    return pl.pallas_call(
        fore_attn_kernel,
        grid=(4,),
        out_shape=(
            jax.ShapeDtypeStruct((SLAB, HEAD, FR), BF),
            jax.ShapeDtypeStruct((4, NKB, QB, QB), BF),
            jax.ShapeDtypeStruct((4, 1, QB), F32),
        ),
        in_specs=[SM, VM, VM, VM],
        out_specs=(PAIR, E_SPEC, I_SPEC),
        scratch_shapes=[
            pltpu.VMEM((NB, HEAD, QB), BF),
            pltpu.VMEM((NB, QB, FR), BF),
            pltpu.VMEM((NKB, QB, QB), F32),
        ],
        cost_estimate=pl.CostEstimate(
            flops=6 * 1024 * 2304 * 128, bytes_accessed=6_000_000, transcendentals=1024 * 2304
        ),
        name="attn_fore",
    )(bounds, own, lo, hi)


def back_attn_kernel(own, lo, hi, do, ctx_i, e_i, inv_i, dq_o, dlo_o, down_o, dhi_o, kt, vn, dkt, dvt):
    step = pl.program_id(0)

    @pl.when(step == 0)
    def _():
        for b in range(24):
            kb, vb = window_block(b, own, lo, hi)
            pair, half = b // 2, b % 2
            cols = slice(half * FR, (half + 1) * FR)
            kt[pair, :, cols] = kb
            vn[pair, cols, :] = jnp.concatenate([vb, jnp.zeros((32, FR), BF)], axis=0).T
        dkt[...] = jnp.zeros_like(dkt)
        dvt[...] = jnp.zeros_like(dvt)

    qt = jnp.concatenate([own[2 * step, 0:HEAD, :], own[2 * step + 1, 0:HEAD, :]], axis=1)
    inverse = inv_i[0]
    ctx = jnp.concatenate([ctx_i[0], ctx_i[1]], axis=1).astype(F32)
    dot_ = jnp.concatenate([do[0], do[1]], axis=1).astype(F32)
    delta = jnp.sum(dot_ * ctx, axis=0, keepdims=True) * inverse
    dos = (dot_ * inverse).astype(BF)
    dosa = jnp.concatenate([dos, jnp.zeros((32, QB), BF)], axis=0)
    dq = jnp.zeros((HEAD, QB), F32)
    nt = (((1,), (1,)), ((), ()))
    for r in range(NKB):
        dp = jnp.dot(vn[step + r], dosa, preferred_element_type=F32)
        weights = e_i[0, r]
        ds = (weights.astype(F32) * (dp - delta)).astype(BF)
        dq = dq + jnp.dot(kt[step + r], ds, preferred_element_type=F32)
        dkt[step + r] += lax.dot_general(qt, ds, nt, preferred_element_type=F32)
        dvt[step + r] += lax.dot_general(dos, weights, nt, preferred_element_type=F32)
    dqb = (dq * SCALE).astype(BF)
    dq_o[0] = dqb[:, :FR]
    dq_o[1] = dqb[:, FR:]

    @pl.when(step == 3)
    def _():
        for b in range(24):
            pair, half = b // 2, b % 2
            cols = slice(half * FR, (half + 1) * FR)
            dk_part = dkt[pair, :, cols] * SCALE
            dv_part = dvt[pair, :, cols]
            ref = (dlo_o, down_o, dhi_o)[b // 8]
            ref[b % 8, 0:HEAD, :] = dk_part.astype(ref.dtype)
            ref[b % 8, HEAD : 2 * HEAD, :] = dv_part.astype(ref.dtype)


def attn_back(own, lo, hi, do, ctx, e, inv):
    return pl.pallas_call(
        back_attn_kernel,
        grid=(4,),
        out_shape=(
            jax.ShapeDtypeStruct((SLAB, HEAD, FR), BF),
            jax.ShapeDtypeStruct((SLAB, 2 * HEAD, FR), BF),
            jax.ShapeDtypeStruct((SLAB, 2 * HEAD, FR), F32),
            jax.ShapeDtypeStruct((SLAB, 2 * HEAD, FR), BF),
        ),
        in_specs=[VM, VM, VM, PAIR, PAIR, E_SPEC, I_SPEC],
        out_specs=(PAIR, VM, VM, VM),
        scratch_shapes=[
            pltpu.VMEM((NB, HEAD, QB), BF),
            pltpu.VMEM((NB, QB, FR), BF),
            pltpu.VMEM((NB, HEAD, QB), F32),
            pltpu.VMEM((NB, HEAD, QB), F32),
        ],
        cost_estimate=pl.CostEstimate(
            flops=8 * 1024 * 2304 * 128, bytes_accessed=8_000_000, transcendentals=0
        ),
        name="attn_back",
    )(own, lo, hi, do, ctx, e, inv)


CW = 512


def fill_ext(ext, prev, mid, nxt):
    ext[0:16, :] = prev[...].astype(F32)
    ext[16:144, :] = mid
    ext[144:160, :] = nxt[...].astype(F32)


def back_kernel(pos, prev, g, nxt, kern, gs_o, tiles_o, ext):
    fill_ext(ext, prev, g[...].astype(F32), nxt)
    rows = pos[0] + lax.broadcasted_iota(jnp.int32, (FR, 128), 0)
    for n in range(CW // 128):
        cols = slice(n * 128, (n + 1) * 128)
        taps = kern[:, cols].astype(F32)
        acc = jnp.zeros((FR, 128), F32)
        for s in range(8):
            moved = ext[s : (160 if s == 0 else s + 152), cols]
            for a in range(5):
                t = 32 - (8 * a + s)
                if 0 <= t < TAPS:
                    acc = acc + taps[t : t + 1, :] * moved[8 * a : 8 * a + FR]
        total = (ext[16:144, cols] + jnp.where(rows < pos[1], acc, 0.0)).astype(BF)
        gs_o[:, cols] = total
        tiles_o[n] = total


def col(rows):
    return pl.BlockSpec((rows, CW), lambda i: (0, i))


def conv_back(pos, prev, g, nxt, kern):
    return pl.pallas_call(
        back_kernel,
        grid=(D // CW,),
        out_shape=(jax.ShapeDtypeStruct((FR, D), BF), jax.ShapeDtypeStruct((12, FR, 128), BF)),
        in_specs=[SM, col(16), col(FR), col(16), col(TAPS)],
        out_specs=(col(FR), pl.BlockSpec((CW // 128, FR, 128), lambda i: (i, 0, 0))),
        scratch_shapes=[pltpu.VMEM((160, CW), F32)],
        cost_estimate=pl.CostEstimate(flops=20_000_000, bytes_accessed=1_300_000, transcendentals=0),
        name="conv_back",
    )(pos, prev, g, nxt, kern)


def fore_kernel(pos, prev, mixed, nxt, g, kern, out_o, gk_o, ext):
    rows = pos[0] + lax.broadcasted_iota(jnp.int32, (FR, CW), 0)
    fill_ext(ext, prev, jnp.where(rows < pos[1], mixed[...], 0.0).astype(BF).astype(F32), nxt)
    for n in range(CW // 128):
        cols = slice(n * 128, (n + 1) * 128)
        taps = kern[:, cols].astype(F32)
        gf = g[:, cols].astype(F32)
        acc = jnp.zeros((FR, 128), F32)
        sums = [None] * TAPS
        for s in range(8):
            moved = ext[s : s + 152, cols]
            for a in range(4):
                t = 8 * a + s
                piece = moved[8 * a : 8 * a + FR]
                acc = acc + taps[t : t + 1, :] * piece
                sums[t] = jnp.sum(gf * piece, axis=0, keepdims=True)
        out_o[:, cols] = (mixed[:, cols] + acc).astype(BF)
        for f in range(4):
            gk_o[f, n] = jnp.concatenate(sums[8 * f : 8 * f + 8], axis=0).astype(BF)


def conv_fore(pos, prev, mixed, nxt, g, kern):
    return pl.pallas_call(
        fore_kernel,
        grid=(D // CW,),
        out_shape=(jax.ShapeDtypeStruct((FR, D), BF), jax.ShapeDtypeStruct((4, 12, 8, 128), BF)),
        in_specs=[SM, col(16), col(FR), col(16), col(FR), col(TAPS)],
        out_specs=(col(FR), pl.BlockSpec((4, CW // 128, 8, 128), lambda i: (0, i, 0, 0))),
        scratch_shapes=[pltpu.VMEM((160, CW), F32)],
        cost_estimate=pl.CostEstimate(flops=40_000_000, bytes_accessed=2_000_000, transcendentals=0),
        name="conv_fore",
    )(pos, prev, mixed, nxt, g, kern)


def outer_kernel(ctx, gs, out):
    acc = jnp.zeros((4 * HEAD, 384), F32)
    for b in range(SLAB):
        left = jnp.concatenate([ctx[h, b] for h in range(4)], axis=0)
        right = jnp.concatenate([gs[b, n] for n in range(3)], axis=1)
        acc = acc + jnp.dot(left, right, preferred_element_type=F32)
    for h in range(4):
        for n in range(3):
            out[h, n] = acc[h * HEAD : (h + 1) * HEAD, n * 128 : (n + 1) * 128].astype(BF)


def outer(ctx, gs):
    return pl.pallas_call(
        outer_kernel,
        out_shape=jax.ShapeDtypeStruct((4, 3, HEAD, 128), BF),
        in_specs=[VM, VM],
        out_specs=VM,
        cost_estimate=pl.CostEstimate(flops=302_000_000, bytes_accessed=1_900_000, transcendentals=0),
        name="outer",
    )(ctx, gs)


def finish_kernel(rows, w_o, k_o):
    for hh in range(2):
        for y in range(4):
            tall = jnp.concatenate([rows[x, hh, y, 0:72, :] for x in range(4)], axis=0).astype(F32)
            for n in range(3):
                at = (3 * y + n) * 128
                w_o[hh * HEAD : (hh + 1) * HEAD, at : at + 128] = tall[n * HEAD : (n + 1) * HEAD]
    for x in range(4):
        acc = jnp.zeros((24, 128), F32)
        for hh in range(2):
            for y in range(4):
                acc = acc + rows[x, hh, y, 72:96, :].astype(F32)
        for n in range(3):
            at = (3 * x + n) * 128
            k_o[:, at : at + 128] = acc[8 * n : 8 * n + 8]


def finish(rows):
    return pl.pallas_call(
        finish_kernel,
        out_shape=(jax.ShapeDtypeStruct((192, D), F32), jax.ShapeDtypeStruct((8, D), F32)),
        in_specs=[VM],
        out_specs=(VM, VM),
        cost_estimate=pl.CostEstimate(flops=0, bytes_accessed=2_000_000, transcendentals=0),
        name="finish",
    )(rows)


def gather_weight(part):
    zh, c = lax.axis_index("zh"), lax.axis_index("c")
    far = lax.ppermute(part, ("zh", "zl"), [(0, 3), (3, 0), (1, 2), (2, 1)])
    first = jnp.where(zh == 0, part, far)
    second = jnp.where(zh == 0, far, part)
    mine = jnp.stack([first, second])
    other = lax.ppermute(mine, "c", [(0, 1), (1, 0)])
    even = jnp.where(c == 0, mine, other)
    odd = jnp.where(c == 0, other, mine)
    blocks = jnp.stack([even, odd], axis=1).reshape(4, 2, HEAD, D)
    return blocks.transpose(1, 0, 2, 3).reshape(HEADS * HEAD, D)


def swap_all(value, axes):
    return lax.all_to_all(value, axes, 0, 0, tiled=True)


def per_device(stream_in, queries, key_proj, values, w_out, conv_kernel, valid_length, grad_out):
    valid = valid_length[0]
    slab = lax.axis_index(("zh", "c", "x"))
    device = lax.axis_index(AX)
    pos = jnp.stack([device * FR, valid]).astype(jnp.int32)
    start = (slab - 1) * 1024
    bounds = jnp.stack([jnp.maximum(0, -start), valid - start]).astype(jnp.int32)
    packed = swap_all(pack(queries, key_proj, values), SL)
    weight_full = gather_weight(w_out)
    kernel_full = swap_all(jnp.broadcast_to(conv_kernel[None], (4, 8, D)), ("zh", "c"))
    kernel_full = kernel_full.reshape(TAPS, D)
    g_prev = shift(grad_out[FR - 16 :], 1)
    g_next = shift(grad_out[:16], -1)
    kv = packed[:, HEAD:, :]
    lo = shift(kv, 8)
    hi = shift(kv, -8)
    grad_stream, tiles = conv_back(pos, g_prev, grad_out, g_next, kernel_full)
    tiles = tiles.reshape(4, 3, FR, 128)
    tiles = swap_all(jnp.concatenate([tiles, tiles], axis=0), SL)
    grad_ctx_t = lax.dot_general(
        weight_full, grad_stream, (((1,), (1,)), ((), ())), preferred_element_type=F32
    ).astype(BF)
    do = swap_all(grad_ctx_t.reshape(HEADS, HEAD, FR), SL)
    ctx, e, inv = attn_fore(bounds, packed, lo, hi)
    ctx_t = swap_all(ctx, SL).reshape(HEADS * HEAD, FR)
    ctx_y = swap_all(jnp.broadcast_to(ctx[None], (4, SLAB, HEAD, FR)), "y")
    dq, dlo, down, dhi = attn_back(packed, lo, hi, do, ctx, e, inv)
    from_hi = shift(dlo, -8)
    from_lo = shift(dhi, 8)
    mixed = stream_in.astype(F32) + lax.dot_general(
        ctx_t, weight_full, (((0,), (0,)), ((), ())), preferred_element_type=F32
    )
    live = (device * FR + jnp.arange(FR, dtype=jnp.int32) < valid)[:, None]
    masked = jnp.where(live, mixed, 0.0).astype(BF)
    m_prev = shift(masked[FR - 16 :], 1)
    m_next = shift(masked[:16], -1)
    term_weight = outer(ctx_y, tiles)
    block_out, term_kernel = conv_fore(pos, m_prev, mixed, m_next, grad_out, kernel_full)
    terms = jnp.concatenate(
        [term_weight.reshape(16, 72, FR), term_kernel.reshape(16, 24, FR)], axis=1
    )
    terms = swap_all(terms, ("zh", "c", "x"))
    grads = (down + from_hi.astype(F32) + from_lo.astype(F32)).astype(BF)
    grads = swap_all(jnp.concatenate([dq, grads], axis=1), SL)
    grad_queries, grad_keys, grad_values = unpack(grads)
    rows = jnp.sum(terms.astype(F32), axis=0).astype(BF)
    rows = swap_all(jnp.broadcast_to(rows[None], (32, 96, FR)), SEQ)
    grad_w_out, grad_kernel = finish(rows.reshape(4, 2, 4, 96, FR))
    return (block_out, grad_stream, grad_queries, grad_keys, grad_values, grad_w_out, grad_kernel)


def solution(mesh):
    fine = Mesh(mesh.devices.reshape(2, 2, 4, 2, 4), AX)
    split = P(AX, None)
    rows = P(("zh", "c"), None)
    return jax.shard_map(
        per_device,
        mesh=fine,
        in_specs=(split, split, split, split, rows, rows, P(), split),
        out_specs=(split, split, split, split, split, rows, rows),
        check_vma=False,
    )
```

time: 217 us -> 205 us (0.945)
  starting transfers between devices: 82.6 us -> 71.1 us
  Pallas kernels: 33.4 us -> 43.7 us
  waiting for transfers between devices: 71.5 us -> 64 us
  local copies, waits for them, and re-layouts: 11.2 us -> 8.55 us
    all_to_all x7 -> x9, waiting for transfers between devices: 63.1 us -> 49.7 us  [swap_all(): return lax.all_to_all(value, axes, 0, 0, tiled=True)]
    ppermute x5 -> x2, waiting for transfers between devices: 0.3 us -> 13.5 us  [the longest x1 13.5 us: gather_weight(): far = lax.ppermute(part, ('zh', 'zl'), [(0, 3), (3, 0), (1, 2), (2, 1)])]
    pallas_call x2 -> x6, Pallas kernels: 22.2 us -> 33.4 us  [the longest x1 12.8 us: attn_back(): pl.pallas_call(back_attn_kernel, grid=(4,), out_shape=(jax.ShapeDtypeStru...]
    ppermute x5 -> x2, starting transfers between devices: 12.8 us -> 4.23 us  [the longest x1 4.23 us: gather_weight(): far = lax.ppermute(part, ('zh', 'zl'), [(0, 3), (3, 0), (1, 2), (2, 1)])]
    ppermute x8, waiting for transfers between devices: 8.12 us -> 0.77 us  [shift(): return lax.ppermute(value, AX, pairs)]
    all_to_all x7 -> x9, starting transfers between devices: 51.1 us -> 46 us  [swap_all(): return lax.all_to_all(value, axes, 0, 0, tiled=True)]
    reshape x9 -> x0, local copies, waits for them, and re-layouts: 4.16 us -> none  [the longest x1 0.83 us: per_device(): grad_keys = grads[:, :HEAD, :].reshape(HEADS * HEAD, FR).T]
    broadcast_in_dim x3, local copies, waits for them, and re-layouts: 0.93 us -> 3.74 us  [the longest x1 1.99 us: per_device(): ctx_y = swap_all(jnp.broadcast_to(ctx[None], (4, SLAB, HEAD, FR)), 'y')]
  transfers between devices with their start and end apart: 20 -> 19, of which waited for: 9 -> 9; matrix products, arithmetic and copies ran while one was open for 6% -> 7% of each run, Pallas kernels for 4% -> 20%
where the time goes in v2:
time: 205 us; the launch traced here: 204 us
  starting transfers between devices  71.1 us (35%)
  waiting for transfers between devices  64 us (31%)
  Pallas kernels  43.7 us (21%)
  other arithmetic  9.91 us (5%)
  local copies, waits for them, and re-layouts  8.55 us (4%)
  matrix products  4.83 us (2%)
    all_to_all x9, waiting for transfers between devices, swap_all(): return lax.all_to_all(value, axes, 0, 0, tiled=True)  49.7 us
    all_to_all x9, starting transfers between devices, swap_all(): return lax.all_to_all(value, axes, 0, 0, tiled=True)  46 us
    ppermute x8, starting transfers between devices, shift(): return lax.ppermute(value, AX, pairs)  20.8 us
    ppermute x1, waiting for transfers between devices, gather_weight(): far = lax.ppermute(part, ('zh', 'zl'), [(0, 3), (3, 0), (1, 2), (2, 1)])  13.5 us
    pallas_call x1, Pallas kernels, attn_back(): pl.pallas_call(back_attn_kernel, grid=(4,), out_shape=(jax.ShapeDtypeStru...  12.8 us
    pallas_call x1, Pallas kernels, attn_fore(): pl.pallas_call(fore_attn_kernel, grid=(4,), out_shape=(jax.ShapeDtypeStru...  8.36 us
    pallas_call x1, Pallas kernels, conv_fore(): pl.pallas_call(fore_kernel, grid=(D // CW,), out_shape=(jax.ShapeDtypeStr...  8.17 us
    pallas_call x1, Pallas kernels, conv_back(): pl.pallas_call(back_kernel, grid=(D // CW,), out_shape=(jax.ShapeDtypeStr...  5.21 us
  transfers between devices with their start and end apart: 19, of which 9 were waited for; matrix products, arithmetic and copies ran while one was open for 7% of the time, Pallas kernels for 20%

profile of v2, /device:TPU:0, one launch (start us, length us, event | category | flops | bytes accessed | tf_op | source)
XLA Modules:
  0.0 203.6 jit_solution(7978783798580315467)
XLA Ops:
  0.6 4.2 %collective-permute-start.2 = (bf16[192,1536]{1,0:T(8,128)(2,1)}, bf16[192,1536]{1,0:T(8,128)(2,1)S(1)}, u32[]{:S(2)}, u32[]{:S(2)}) collective-permute-start(bf16[192,1536]{1,0:T(8,128)(2,1)} %param.12), channel_id=1, source_target_pairs={{0,68},{68,0},{4,64},{64,4},{1,69},{69,1},{5,65},{65,5},{2,70},{70... | collective-permute-start | bytes 1769480 | tf_op jit(solution)/shard_map/ppermute | solution.py:360
  4.9 13.5 %collective-permute-done.2 = bf16[192,1536]{1,0:T(8,128)(2,1)S(1)} collective-permute-done((bf16[192,1536]{1,0:T(8,128)(2,1)}, bf16[192,1536]{1,0:T(8,128)(2,1)S(1)}, u32[]{:S(2)}, u32[]{:S(2)}) %collective-permute-start.2) | collective-permute-done | bytes 589856 | tf_op jit(solution)/shard_map/ppermute | solution.py:360
  18.4 1.1 select_bitcast_fusion.3
  19.5 1.1 pad_maximum_fusion.1
  20.7 0.0 collective-permute-start.3
  20.7 2.1 %pack.1 = bf16[8,288,128]{2,1,0:T(8,128)(2,1)} custom-call(bf16[128,768]{1,0:T(8,128)(2,1)} %q.1, bf16[128,768]{1,0:T(8,128)(2,1)} %k.1, bf16[128,768]{1,0:T(8,128)(2,1)} %v.1), custom_call_target="tpu_custom_call" | custom-call | bytes 1200000 | tf_op jit(solution)/shard_map/pack/pallas_call | solution.py:47
  22.8 4.5 %all-to-all-start = ((bf16[8,288,128]{2,1,0:T(8,128)(2,1)}), bf16[8,288,128]{2,1,0:T(8,128)(2,1)S(1)}, u32[]{:S(2)}, u32[]{:S(2)}) async-start(bf16[8,288,128]{2,1,0:T(8,128)(2,1)} %pack.1), calls=%async_computation | async-start | bytes 1179648 | tf_op jit(solution)/shard_map/all_to_all | solution.py:372
  27.3 0.8 fusion
  28.1 3.9 %collective-permute-start.6 = (bf16[16,1536]{1,0:T(8,128)(2,1)S(1)}, bf16[16,1536]{1,0:T(8,128)(2,1)S(1)}, u32[]{:S(2)}, u32[]{:S(2)}) collective-permute-start(bf16[16,1536]{1,0:T(8,128)(2,1)S(1)} %get-tuple-element.44), channel_id=1, source_target_pairs={{0,1},{1,2},{2,3},{3,4},{4,5},{5,6},{6,7},{7,8},{8,9},{9,10},{10,1... | collective-permute-start | bytes 147464 | tf_op jit(solution)/shard_map/ppermute | solution.py:33
  32.0 1.3 collective-permute-start.7
  34.0 5.8 %all-to-all-done.own = bf16[8,288,128]{2,1,0:T(8,128)(2,1)S(1)} async-done(((bf16[8,288,128]{2,1,0:T(8,128)(2,1)}), bf16[8,288,128]{2,1,0:T(8,128)(2,1)S(1)}, u32[]{:S(2)}, u32[]{:S(2)}) %all-to-all-start) | async-done | bytes 589856 | tf_op jit(solution)/shard_map/all_to_all | solution.py:372
  39.8 0.7 broadcast_in_dim.20
  40.5 4.6 %all-to-all-start.2 = ((bf16[4,8,1536]{2,1,0:T(8,128)(2,1)}), bf16[4,8,1536]{2,1,0:T(8,128)(2,1)S(1)}, u32[]{:S(2)}, u32[]{:S(2)}) async-start(bf16[4,8,1536]{2,1,0:T(8,128)(2,1)} %broadcast_in_dim.20), calls=%async_computation.2 | async-start | bytes 196608 | tf_op jit(solution)/shard_map/all_to_all | solution.py:372
  45.1 4.7 %collective-permute-start = (bf16[8,192,128]{2,1,0:T(8,128)(2,1)S(1)}, bf16[8,192,128]{2,1,0:T(8,128)(2,1)}, u32[]{:S(2)}, u32[]{:S(2)}) collective-permute-start(bf16[8,192,128]{2,1,0:T(8,128)(2,1)S(1)} %slice.20), channel_id=1, source_target_pairs={{0,8},{1,9},{2,10},{3,11},{4,12},{5,13},{6,14},{7,15},{8,16},{9,17... | collective-permute-start | bytes 1179656 | tf_op jit(solution)/shard_map/ppermute | solution.py:33
  49.8 1.3 collective-permute-start.1
  51.1 0.7 pad_add_fusion.pos
  51.8 0.6 pad_add_fusion.1.bounds
  52.3 0.0 collective-permute-done.7.nxt
  52.3 0.0 copy-start.13
  52.4 0.6 copy-done.12
  52.9 0.0 copy-done.13
  53.0 0.0 copy-done.6
  53.0 5.2 %conv_back.1 = (bf16[128,1536]{1,0:T(8,128)(2,1)}, bf16[12,128,128]{2,1,0:T(8,128)(2,1)}) custom-call(s32[2]{0:T(128)} %pad_add_fusion.pos, bf16[16,1536]{1,0:T(8,128)(2,1)} %copy-done.12, bf16[128,1536]{1,0:T(8,128)(2,1)} %g.3, bf16[16,1536]{1,0:T(8,128)(2,1)} %copy-done.13, bf16[32,1536]{1,0:T(8,128)(2,1)} %bitcast.36), custom_call_target="tpu_custom_call" | custom-call | flops 20000000 | bytes 1300000 | tf_op jit(solution)/shard_map/conv_back/pallas_call | solution.py:262
  58.2 2.1 %pad_maximum_fusion.2 = bf16[8,3,128,128]{3,2,1,0:T(8,128)(2,1)} fusion(bf16[4,3,128,128]{3,2,1,0:T(8,128)(2,1)} %bitcast.39), kind=kLoop, calls=%fused_computation.6 | loop fusion | flops 393216 | bytes 1179648 | tf_op jit(solution)/shard_map/concatenate | solution.py:393
  60.3 3.5 %all-to-all-start.6 = ((bf16[8,3,128,128]{3,2,1,0:T(8,128)(2,1)}), bf16[8,3,128,128]{3,2,1,0:T(8,128)(2,1)S(1)}, u32[]{:S(2)}, u32[]{:S(2)}) async-start(bf16[8,3,128,128]{3,2,1,0:T(8,128)(2,1)} %pad_maximum_fusion.2), calls=%async_computation.6 | async-start | bytes 1572864 | tf_op jit(solution)/shard_map/all_to_all | solution.py:372
  63.8 8.4 %attn_fore.1 = (bf16[8,96,128]{2,1,0:T(8,128)(2,1)}, bf16[4,9,256,256]{3,2,1,0:T(8,128)(2,1)}, f32[4,1,256]{2,1,0:T(1,128)}) custom-call(s32[2]{0:T(128)} %pad_add_fusion.1.bounds, bf16[8,288,128]{2,1,0:T(8,128)(2,1)} %copy-done.4, bf16[8,192,128]{2,1,0:T(8,128)(2,1)} %collective-permute-done.lo, bf16[8,192,128]{2,1,0:T(8,128)(2,1)} %collective-permute-done.1.hi), custom_call_target="tpu_custom_call" | custom-call | flops 1811939328 | bytes 6000000 | tf_op jit(solution)/shard_map/attn_fore/pallas_call | solution.py:137
  72.2 1.4 select_bitcast_fusion.1
  73.6 0.2 pad_maximum_fusion
  73.9 0.2 copy.16
  74.0 3.7 %all-to-all-done.6.gs = bf16[8,3,128,128]{3,2,1,0:T(8,128)(2,1)S(1)} async-done(((bf16[8,3,128,128]{3,2,1,0:T(8,128)(2,1)}), bf16[8,3,128,128]{3,2,1,0:T(8,128)(2,1)S(1)}, u32[]{:S(2)}, u32[]{:S(2)}) %all-to-all-start.6) | async-done | bytes 786464 | tf_op jit(solution)/shard_map/all_to_all | solution.py:372
  77.7 3.4 %all-to-all-start.1 = ((bf16[8,96,128]{2,1,0:T(8,128)(2,1)}), bf16[8,96,128]{2,1,0:T(8,128)(2,1)S(1)}, u32[]{:S(2)}, u32[]{:S(2)}) async-start(bf16[8,96,128]{2,1,0:T(8,128)(2,1)} %get-tuple-element.23.ctx_i), calls=%async_computation.1 | async-start | bytes 393216 | tf_op jit(solution)/shard_map/all_to_all | solution.py:372
  81.1 2.4 %convolution_convert_fusion = bf16[768,128]{1,0:T(8,128)(2,1)} fusion(bf16[768,1536]{1,0:T(8,128)(2,1)S(1)} %bitcast.31, bf16[128,1536]{1,0:T(8,128)(2,1)} %get-tuple-element.17), kind=kOutput, calls=%fused_computation.5 | convolution fusion | flops 302088192 | bytes 2949120 | tf_op jit(solution)/shard_map/dot_general | solution.py:394
  83.6 4.6 %all-to-all-done.1 = bf16[8,96,128]{2,1,0:T(8,128)(2,1)S(1)} async-done(((bf16[8,96,128]{2,1,0:T(8,128)(2,1)}), bf16[8,96,128]{2,1,0:T(8,128)(2,1)S(1)}, u32[]{:S(2)}, u32[]{:S(2)}) %all-to-all-start.1) | async-done | bytes 196640 | tf_op jit(solution)/shard_map/all_to_all | solution.py:372
  88.2 3.4 %all-to-all-start.3 = ((bf16[8,96,128]{2,1,0:T(8,128)(2,1)}), bf16[8,96,128]{2,1,0:T(8,128)(2,1)S(1)}, u32[]{:S(2)}, u32[]{:S(2)}) async-start(bf16[8,96,128]{2,1,0:T(8,128)(2,1)} %bitcast.14), calls=%async_computation.3 | async-start | bytes 393216 | tf_op jit(solution)/shard_map/all_to_all | solution.py:372
  91.6 2.4 %select_convert_fusion = (bf16[128,1536]{1,0:T(8,128)(2,1)S(1)}, f32[128,1536]{1,0:T(8,128)}) fusion(pred[128]{0:T(512)(128)(4,1)S(1)} %add_compare_fusion, bf16[768,128]{1,0:T(8,128)(2,1)S(1)} %bitcast.38, bf16[768,1536]{1,0:T(8,128)(2,1)S(1)} %bitcast.32, bf16[128,1536]{1,0:T(8,128)(2,1)} %param.8), kind=kOutput, calls=%fused_computation.8 | convolution fusion | flops 302579712 | bytes 4128896 | tf_op jit(solution)/shard_map/dot_general | solution.py:404
  94.0 4.5 %all-to-all-done.3.do = bf16[8,96,128]{2,1,0:T(8,128)(2,1)S(1)} async-done(((bf16[8,96,128]{2,1,0:T(8,128)(2,1)}), bf16[8,96,128]{2,1,0:T(8,128)(2,1)S(1)}, u32[]{:S(2)}, u32[]{:S(2)}) %all-to-all-start.3) | async-done | bytes 196640 | tf_op jit(solution)/shard_map/all_to_all | solution.py:372
  98.5 2.0 broadcast_in_dim.34
  100.5 3.5 %all-to-all-start.5 = ((bf16[4,8,96,128]{3,2,1,0:T(8,128)(2,1)}), bf16[4,8,96,128]{3,2,1,0:T(8,128)(2,1)S(1)}, u32[]{:S(2)}, u32[]{:S(2)}) async-start(bf16[4,8,96,128]{3,2,1,0:T(8,128)(2,1)} %broadcast_in_dim.34), calls=%async_computation.5 | async-start | bytes 1572864 | tf_op jit(solution)/shard_map/all_to_all | solution.py:372
  104.0 12.8 %attn_back.1 = (bf16[8,96,128]{2,1,0:T(8,128)(2,1)}, bf16[8,192,128]{2,1,0:T(8,128)(2,1)}, f32[8,192,128]{2,1,0:T(8,128)}, bf16[8,192,128]{2,1,0:T(8,128)(2,1)}) custom-call(bf16[8,288,128]{2,1,0:T(8,128)(2,1)} %copy-done.4, bf16[8,192,128]{2,1,0:T(8,128)(2,1)} %collective-permute-done.lo, bf16[8,192,128]{2,1,0:T(8,128)(2,1)} %collective-permute-done.1.hi, ...), custom_call_target="tpu_custom_call" | custom-call | flops 2415919104 | bytes 8000000 | tf_op jit(solution)/shard_map/attn_back/pallas_call | solution.py:206
  116.8 2.9 %collective-permute-start.9 = (bf16[8,192,128]{2,1,0:T(8,128)(2,1)}, bf16[8,192,128]{2,1,0:T(8,128)(2,1)S(1)}, u32[]{:S(2)}, u32[]{:S(2)}) collective-permute-start(bf16[8,192,128]{2,1,0:T(8,128)(2,1)} %get-tuple-element.31), channel_id=1, source_target_pairs={{0,8},{1,9},{2,10},{3,11},{4,12},{5,13},{6,14},{7,15},{8,16},{9,17... | collective-permute-start | bytes 1179656 | tf_op jit(solution)/shard_map/ppermute | solution.py:33
  119.7 1.3 collective-permute-start.8
  121.0 3.9 %collective-permute-start.4 = (bf16[16,1536]{1,0:T(8,128)(2,1)S(1)}, bf16[16,1536]{1,0:T(8,128)(2,1)S(1)}, u32[]{:S(2)}, u32[]{:S(2)}) collective-permute-start(bf16[16,1536]{1,0:T(8,128)(2,1)S(1)} %get-tuple-element.46), channel_id=1, source_target_pairs={{0,1},{1,2},{2,3},{3,4},{4,5},{5,6},{6,7},{7,8},{8,9},{9,10},{10,1... | collective-permute-start | bytes 147464 | tf_op jit(solution)/shard_map/ppermute | solution.py:33
  124.9 1.5 collective-permute-start.5
  126.4 0.9 copy-done.1
  127.3 2.8 %outer.1 = bf16[4,3,96,128]{3,2,1,0:T(8,128)(2,1)} custom-call(bf16[4,8,96,128]{3,2,1,0:T(8,128)(2,1)} %copy-done.1, bf16[8,3,128,128]{3,2,1,0:T(8,128)(2,1)} %copy-done), custom_call_target="tpu_custom_call" | custom-call | flops 302000000 | bytes 1900000 | tf_op jit(solution)/shard_map/outer/pallas_call | solution.py:320
  130.1 0.7 collective-permute-done.5.nxt
  130.9 0.6 copy-done.11
  131.5 8.2 %conv_fore.1 = (bf16[128,1536]{1,0:T(8,128)(2,1)}, bf16[4,12,8,128]{3,2,1,0:T(8,128)(2,1)}) custom-call(s32[2]{0:T(128)} %pad_add_fusion.pos, bf16[16,1536]{1,0:T(8,128)(2,1)} %copy-done.10, f32[128,1536]{1,0:T(8,128)} %get-tuple-element.48.mixed, bf16[16,1536]{1,0:T(8,128)(2,1)} %copy-done.11, bf16[128,1536]{1,0:T(8,128)(2,1)} %g.3, bf16[32,1536]{1,0:T(8,128)(2,1)} %bitcast.37), custom_call_target="tpu_custom_call" | custom-call | flops 40000000 | bytes 2000000 | tf_op jit(solution)/shard_map/conv_fore/pallas_call | solution.py:296
  139.7 1.7 pad_maximum_fusion.4
  141.4 15.3 %all-to-all-start.7 = ((bf16[16,96,128]{2,1,0:T(8,128)(2,1)}), bf16[16,96,128]{2,1,0:T(8,128)(2,1)S(1)}, u32[]{:S(2)}, u32[]{:S(2)}) async-start(bf16[16,96,128]{2,1,0:T(8,128)(2,1)} %pad_maximum_fusion.4), calls=%async_computation.7 | async-start | bytes 786432 | tf_op jit(solution)/shard_map/all_to_all | solution.py:372
  156.7 0.0 copy-start.8
  156.7 0.1 add_convert_fusion
  156.9 0.7 copy-done.8
  157.6 0.9 pad_maximum_fusion.3
  158.5 8.9 %all-to-all-done.7 = bf16[16,96,128]{2,1,0:T(8,128)(2,1)S(1)} async-done(((bf16[16,96,128]{2,1,0:T(8,128)(2,1)}), bf16[16,96,128]{2,1,0:T(8,128)(2,1)S(1)}, u32[]{:S(2)}, u32[]{:S(2)}) %all-to-all-start.7) | async-done | bytes 393248 | tf_op jit(solution)/shard_map/all_to_all | solution.py:372
  167.4 3.5 %all-to-all-start.4 = ((bf16[8,288,128]{2,1,0:T(8,128)(2,1)}), bf16[8,288,128]{2,1,0:T(8,128)(2,1)S(1)}, u32[]{:S(2)}, u32[]{:S(2)}) async-start(bf16[8,288,128]{2,1,0:T(8,128)(2,1)} %pad_maximum_fusion.3), calls=%async_computation.4 | async-start | bytes 1179648 | tf_op jit(solution)/shard_map/all_to_all | solution.py:372
  170.9 0.1 reduce_sum.12
  171.0 10.4 %all-to-all-done.4.got = bf16[8,288,128]{2,1,0:T(8,128)(2,1)S(1)} async-done(((bf16[8,288,128]{2,1,0:T(8,128)(2,1)}), bf16[8,288,128]{2,1,0:T(8,128)(2,1)S(1)}, u32[]{:S(2)}, u32[]{:S(2)}) %all-to-all-start.4) | async-done | bytes 589856 | tf_op jit(solution)/shard_map/all_to_all | solution.py:372
  181.3 1.1 broadcast_in_dim.35
  182.4 4.3 %all-to-all-start.8 = ((bf16[32,96,128]{2,1,0:T(8,128)(2,1)}), bf16[32,96,128]{2,1,0:T(8,128)(2,1)S(1)}, u32[]{:S(2)}, u32[]{:S(2)}) async-start(bf16[32,96,128]{2,1,0:T(8,128)(2,1)} %broadcast_in_dim.35), calls=%async_computation.8 | async-start | bytes 1572864 | tf_op jit(solution)/shard_map/all_to_all | solution.py:372
  186.7 2.0 unpack.1
  188.7 11.8 %all-to-all-done.8 = bf16[32,96,128]{2,1,0:T(8,128)(2,1)S(1)} async-done(((bf16[32,96,128]{2,1,0:T(8,128)(2,1)}), bf16[32,96,128]{2,1,0:T(8,128)(2,1)S(1)}, u32[]{:S(2)}, u32[]{:S(2)}) %all-to-all-start.8) | async-done | bytes 786464 | tf_op jit(solution)/shard_map/all_to_all | solution.py:372
  200.5 0.9 copy-done.2
  201.4 2.2 %finish.1 = (f32[192,1536]{1,0:T(8,128)}, f32[8,1536]{1,0:T(8,128)}) custom-call(bf16[4,2,4,96,128]{4,3,2,1,0:T(8,128)(2,1)} %bitcast.34), custom_call_target="tpu_custom_call" | custom-call | bytes 2000000 | tf_op jit(solution)/shard_map/finish/pallas_call | solution.py:348
  (33 shorter events, 0.1 us)
Async XLA Ops:
  0.6 17.8 %collective-permute-start.2 = (bf16[192,1536]{1,0:T(8,128)(2,1)}, bf16[192,1536]{1,0:T(8,128)(2,1)S(1)}, u32[]{:S(2)}, u32[]{:S(2)}) collective-permute-start(bf16[192,1536]{1,0:T(8,128)(2,1)} %param.12), channel_id=1, source_target_pairs={{0,68},{68,0},{4,64},{64,4},{1,69},{69,1},{5,65},{65,5},{2,70},{70... | collective-permute-start | bytes 1769480 | tf_op jit(solution)/shard_map/ppermute | solution.py:360
  20.7 19.1 %copy-start.14 = (bf16[8,1536]{1,0:T(8,128)(2,1)S(1)}, bf16[8,1536]{1,0:T(8,128)(2,1)}, u32[]{:S(2)}) copy-start(bf16[8,1536]{1,0:T(8,128)(2,1)} %param.13) | copy-start | bytes 73732
  20.7 51.5 %collective-permute-start.3 = (bf16[2,192,1536]{2,1,0:T(8,128)(2,1)}, bf16[2,192,1536]{2,1,0:T(8,128)(2,1)}, u32[]{:S(2)}, u32[]{:S(2)}) collective-permute-start(bf16[2,192,1536]{2,1,0:T(8,128)(2,1)} %pad_maximum_fusion.1), channel_id=1, source_target_pairs={{0,32},{32,0},{1,33},{33,1},{2,34},{34,2},{3,35},{35,3},{4,36},{36... | collective-permute-start | bytes 3538952 | tf_op jit(solution)/shard_map/ppermute | solution.py:364
  22.8 17.0 %all-to-all-start = ((bf16[8,288,128]{2,1,0:T(8,128)(2,1)}), bf16[8,288,128]{2,1,0:T(8,128)(2,1)S(1)}, u32[]{:S(2)}, u32[]{:S(2)}) async-start(bf16[8,288,128]{2,1,0:T(8,128)(2,1)} %pack.1), calls=%async_computation | async-start | bytes 1179648 | tf_op jit(solution)/shard_map/all_to_all | solution.py:372
  28.1 24.2 %collective-permute-start.6 = (bf16[16,1536]{1,0:T(8,128)(2,1)S(1)}, bf16[16,1536]{1,0:T(8,128)(2,1)S(1)}, u32[]{:S(2)}, u32[]{:S(2)}) collective-permute-start(bf16[16,1536]{1,0:T(8,128)(2,1)S(1)} %get-tuple-element.44), channel_id=1, source_target_pairs={{0,1},{1,2},{2,3},{3,4},{4,5},{5,6},{6,7},{7,8},{8,9},{9,10},{10,1... | collective-permute-start | bytes 147464 | tf_op jit(solution)/shard_map/ppermute | solution.py:33
  32.0 20.3 %collective-permute-start.7 = (bf16[16,1536]{1,0:T(8,128)(2,1)S(1)}, bf16[16,1536]{1,0:T(8,128)(2,1)S(1)}, u32[]{:S(2)}, u32[]{:S(2)}) collective-permute-start(bf16[16,1536]{1,0:T(8,128)(2,1)S(1)} %get-tuple-element.43), channel_id=1, source_target_pairs={{1,0},{2,1},{3,2},{4,3},{5,4},{6,5},{7,6},{8,7},{9,8},{10,9},{11,1... | collective-permute-start | bytes 147464 | tf_op jit(solution)/shard_map/ppermute | solution.py:33
  39.8 20.5 %copy-start.4 = (bf16[8,288,128]{2,1,0:T(8,128)(2,1)}, bf16[8,288,128]{2,1,0:T(8,128)(2,1)S(1)}, u32[]{:S(2)}) copy-start(bf16[8,288,128]{2,1,0:T(8,128)(2,1)S(1)} %all-to-all-done.own) | copy-start | bytes 1769476
  40.5 11.9 %all-to-all-start.2 = ((bf16[4,8,1536]{2,1,0:T(8,128)(2,1)}), bf16[4,8,1536]{2,1,0:T(8,128)(2,1)S(1)}, u32[]{:S(2)}, u32[]{:S(2)}) async-start(bf16[4,8,1536]{2,1,0:T(8,128)(2,1)} %broadcast_in_dim.20), calls=%async_computation.2 | async-start | bytes 196608 | tf_op jit(solution)/shard_map/all_to_all | solution.py:372
  45.1 18.7 %collective-permute-start = (bf16[8,192,128]{2,1,0:T(8,128)(2,1)S(1)}, bf16[8,192,128]{2,1,0:T(8,128)(2,1)}, u32[]{:S(2)}, u32[]{:S(2)}) collective-permute-start(bf16[8,192,128]{2,1,0:T(8,128)(2,1)S(1)} %slice.20), channel_id=1, source_target_pairs={{0,8},{1,9},{2,10},{3,11},{4,12},{5,13},{6,14},{7,15},{8,16},{9,17... | collective-permute-start | bytes 1179656 | tf_op jit(solution)/shard_map/ppermute | solution.py:33
  49.8 14.0 %collective-permute-start.1 = (bf16[8,192,128]{2,1,0:T(8,128)(2,1)S(1)}, bf16[8,192,128]{2,1,0:T(8,128)(2,1)}, u32[]{:S(2)}, u32[]{:S(2)}) collective-permute-start(bf16[8,192,128]{2,1,0:T(8,128)(2,1)S(1)} %slice.20), channel_id=1, source_target_pairs={{8,0},{9,1},{10,2},{11,3},{12,4},{13,5},{14,6},{15,7},{16,8},{17,9... | collective-permute-start | bytes 1179656 | tf_op jit(solution)/shard_map/ppermute | solution.py:33
  52.3 0.6 copy-start.12
  52.3 0.6 copy-start.13
  52.3 0.6 copy-start.6
  60.3 17.5 %all-to-all-start.6 = ((bf16[8,3,128,128]{3,2,1,0:T(8,128)(2,1)}), bf16[8,3,128,128]{3,2,1,0:T(8,128)(2,1)S(1)}, u32[]{:S(2)}, u32[]{:S(2)}) async-start(bf16[8,3,128,128]{3,2,1,0:T(8,128)(2,1)} %pad_maximum_fusion.2), calls=%async_computation.6 | async-start | bytes 1572864 | tf_op jit(solution)/shard_map/all_to_all | solution.py:372
  77.7 5.9 %copy-start = (bf16[8,3,128,128]{3,2,1,0:T(8,128)(2,1)}, bf16[8,3,128,128]{3,2,1,0:T(8,128)(2,1)S(1)}, u32[]{:S(2)}) copy-start(bf16[8,3,128,128]{3,2,1,0:T(8,128)(2,1)S(1)} %all-to-all-done.6.gs) | copy-start | bytes 2359300
  77.7 10.5 %all-to-all-start.1 = ((bf16[8,96,128]{2,1,0:T(8,128)(2,1)}), bf16[8,96,128]{2,1,0:T(8,128)(2,1)S(1)}, u32[]{:S(2)}, u32[]{:S(2)}) async-start(bf16[8,96,128]{2,1,0:T(8,128)(2,1)} %get-tuple-element.23.ctx_i), calls=%async_computation.1 | async-start | bytes 393216 | tf_op jit(solution)/shard_map/all_to_all | solution.py:372
  88.2 10.3 %all-to-all-start.3 = ((bf16[8,96,128]{2,1,0:T(8,128)(2,1)}), bf16[8,96,128]{2,1,0:T(8,128)(2,1)S(1)}, u32[]{:S(2)}, u32[]{:S(2)}) async-start(bf16[8,96,128]{2,1,0:T(8,128)(2,1)} %bitcast.14), calls=%async_computation.3 | async-start | bytes 393216 | tf_op jit(solution)/shard_map/all_to_all | solution.py:372
  98.5 2.0 copy-start.9
  100.5 25.9 %all-to-all-start.5 = ((bf16[4,8,96,128]{3,2,1,0:T(8,128)(2,1)}), bf16[4,8,96,128]{3,2,1,0:T(8,128)(2,1)S(1)}, u32[]{:S(2)}, u32[]{:S(2)}) async-start(bf16[4,8,96,128]{3,2,1,0:T(8,128)(2,1)} %broadcast_in_dim.34), calls=%async_computation.5 | async-start | bytes 1572864 | tf_op jit(solution)/shard_map/all_to_all | solution.py:372
  116.8 39.9 %collective-permute-start.9 = (bf16[8,192,128]{2,1,0:T(8,128)(2,1)}, bf16[8,192,128]{2,1,0:T(8,128)(2,1)S(1)}, u32[]{:S(2)}, u32[]{:S(2)}) collective-permute-start(bf16[8,192,128]{2,1,0:T(8,128)(2,1)} %get-tuple-element.31), channel_id=1, source_target_pairs={{0,8},{1,9},{2,10},{3,11},{4,12},{5,13},{6,14},{7,15},{8,16},{9,17... | collective-permute-start | bytes 1179656 | tf_op jit(solution)/shard_map/ppermute | solution.py:33
  119.7 37.0 %collective-permute-start.8 = (bf16[8,192,128]{2,1,0:T(8,128)(2,1)}, bf16[8,192,128]{2,1,0:T(8,128)(2,1)S(1)}, u32[]{:S(2)}, u32[]{:S(2)}) collective-permute-start(bf16[8,192,128]{2,1,0:T(8,128)(2,1)} %get-tuple-element.30), channel_id=1, source_target_pairs={{8,0},{9,1},{10,2},{11,3},{12,4},{13,5},{14,6},{15,7},{16,8},{17,9... | collective-permute-start | bytes 1179656 | tf_op jit(solution)/shard_map/ppermute | solution.py:33
  121.0 9.1 %collective-permute-start.4 = (bf16[16,1536]{1,0:T(8,128)(2,1)S(1)}, bf16[16,1536]{1,0:T(8,128)(2,1)S(1)}, u32[]{:S(2)}, u32[]{:S(2)}) collective-permute-start(bf16[16,1536]{1,0:T(8,128)(2,1)S(1)} %get-tuple-element.46), channel_id=1, source_target_pairs={{0,1},{1,2},{2,3},{3,4},{4,5},{5,6},{6,7},{7,8},{8,9},{9,10},{10,1... | collective-permute-start | bytes 147464 | tf_op jit(solution)/shard_map/ppermute | solution.py:33
  124.9 6.0 %collective-permute-start.5 = (bf16[16,1536]{1,0:T(8,128)(2,1)S(1)}, bf16[16,1536]{1,0:T(8,128)(2,1)S(1)}, u32[]{:S(2)}, u32[]{:S(2)}) collective-permute-start(bf16[16,1536]{1,0:T(8,128)(2,1)S(1)} %get-tuple-element.45), channel_id=1, source_target_pairs={{1,0},{2,1},{3,2},{4,3},{5,4},{6,5},{7,6},{8,7},{9,8},{10,9},{11,1... | collective-permute-start | bytes 147464 | tf_op jit(solution)/shard_map/ppermute | solution.py:33
  126.4 0.9 copy-start.1
  130.1 9.6 %copy-start.5 = (bf16[4,3,96,128]{3,2,1,0:T(8,128)(2,1)S(1)}, bf16[4,3,96,128]{3,2,1,0:T(8,128)(2,1)}, u32[]{:S(2)}) copy-start(bf16[4,3,96,128]{3,2,1,0:T(8,128)(2,1)} %outer.1) | copy-start | bytes 884740
  130.1 0.8 copy-start.10
  130.9 0.6 copy-start.11
  131.5 25.2 %copy-start.7 = (f32[8,192,128]{2,1,0:T(8,128)S(1)}, f32[8,192,128]{2,1,0:T(8,128)}, u32[]{:S(2)}) copy-start(f32[8,192,128]{2,1,0:T(8,128)} %get-tuple-element.29) | copy-start | bytes 2359300
  141.4 26.0 %all-to-all-start.7 = ((bf16[16,96,128]{2,1,0:T(8,128)(2,1)}), bf16[16,96,128]{2,1,0:T(8,128)(2,1)S(1)}, u32[]{:S(2)}, u32[]{:S(2)}) async-start(bf16[16,96,128]{2,1,0:T(8,128)(2,1)} %pad_maximum_fusion.4), calls=%async_computation.7 | async-start | bytes 786432 | tf_op jit(solution)/shard_map/all_to_all | solution.py:372
  156.7 0.9 copy-start.8
  167.4 14.0 %all-to-all-start.4 = ((bf16[8,288,128]{2,1,0:T(8,128)(2,1)}), bf16[8,288,128]{2,1,0:T(8,128)(2,1)S(1)}, u32[]{:S(2)}, u32[]{:S(2)}) async-start(bf16[8,288,128]{2,1,0:T(8,128)(2,1)} %pad_maximum_fusion.3), calls=%async_computation.4 | async-start | bytes 1179648 | tf_op jit(solution)/shard_map/all_to_all | solution.py:372
  181.3 1.1 copy-start.3
  182.4 18.1 %all-to-all-start.8 = ((bf16[32,96,128]{2,1,0:T(8,128)(2,1)}), bf16[32,96,128]{2,1,0:T(8,128)(2,1)S(1)}, u32[]{:S(2)}, u32[]{:S(2)}) async-start(bf16[32,96,128]{2,1,0:T(8,128)(2,1)} %broadcast_in_dim.35), calls=%async_computation.8 | async-start | bytes 1572864 | tf_op jit(solution)/shard_map/all_to_all | solution.py:372
  200.5 0.9 copy-start.2
